TPU v7x, 32 devices: a whole 2x2x4 slice. The times are simulated.
32 devices in a mesh: seq: 8 (over z, y), section: 4 (over x, core).
Axes of the slice: x: 2, y: 2, z: 4, core: 2. Of those that a mesh axis runs over, the one named last changes fastest.
Arguments:
- queries: bfloat16 [4, 1024, 2048], P('section', 'seq'), may hold values from -6 to 6
- key_vectors: bfloat16 [4, 1024, 2048], P('section', 'seq'), may hold values from -6 to 6
- value_vectors: bfloat16 [4, 1024, 2048], P('section', 'seq'), may hold values from -6 to 6
- log_decay: bfloat16 [4, 1024, 2048], P('section', 'seq'), may hold values from -0.7 to 0, as said below
- write_strength: float32 [4, 16, 1024], P('section', None, 'seq'), may hold values from 0.1 to 0.9
- out_gain: float32 [4, 2048], P('section'), may hold values from 0.1 to 1.9
- out_weight: bfloat16 [4, 2048, 2304], P('section', None, 'seq'), may hold values from -0.125 to 0.125
Outputs:
- next_input: bfloat16 [4, 1024, 2304], P('section', 'seq')
Inputs may be any that keep to these rules, and one draw needn't show every extreme that they name: `log_decay`: every entry is negative.
All inputs are finite; a program needn't handle non-finite values.
Results may differ from a plain program's by a relative error of at most 0.0051.
Values may be sent and summed in bfloat16 or wider, within the bound.
No kernel may reach another device: no remote copies, remote signals or barrier semaphores. Data moves between devices by JAX's collectives and lax.ppermute only.
A program may use at most 192 MiB of HBM per device.

v0:
```python
import jax
import jax.numpy as jnp
from jax import lax
from jax.sharding import PartitionSpec as P

GROUP = 64


exact_precision = lax.Precision.HIGHEST


def prefix_2(shard, axis, combine, identity):
    devices, position = (lax.axis_size(axis), lax.axis_index(axis))
    everything = jax.tree.map(lambda part: lax.all_gather(part, axis), shard)
    start = jax.tree.map(
        lambda part, zero: jnp.broadcast_to(jnp.asarray(zero, part.dtype), part.shape),
        shard,
        identity,
    )

    def turn(k, before):
        reached = k < position
        new = combine(before, jax.tree.map(lambda part: part[k], everything))
        return jax.tree.map(lambda a, b: jnp.where(reached, a, b), new, before)

    return lax.fori_loop(0, devices, turn, start)


def shifted(value, axis, steps):
    count = lax.axis_size(axis)
    pairs = [(source, (source + steps) % count) for source in range(count)]
    return lax.ppermute(value, axis, pairs)


def unit_rows(values):
    return values * lax.rsqrt(jnp.sum(values * values, axis=-1, keepdims=True) + 1e-06)


def prepare(query_block, key_unit, value_block, decay_block, strength):
    length = decay_block.shape[-2]
    cumulative = jnp.cumsum(decay_block, axis=-2)
    grown = jnp.exp(cumulative)
    shrunk = jnp.exp(-cumulative)
    end_decay = grown[..., -1:, :]
    key_grown = key_unit * grown
    key_shrunk = key_unit * shrunk
    query_grown = query_block * grown
    row_index = lax.broadcasted_iota(jnp.int32, (length, length), 0)
    col_index = lax.broadcasted_iota(jnp.int32, (length, length), 1)
    strict_lower = (row_index > col_index).astype(jnp.float32)
    with_diagonal = (row_index >= col_index).astype(jnp.float32)
    weight_row = strength[..., None, :]
    key_mix = (
        jnp.einsum("...id,...jd->...ij", key_grown, key_shrunk, precision=exact_precision)
        * strict_lower
        * weight_row
    )
    unit_lower = key_mix + jnp.eye(length, dtype=jnp.float32)
    solved_values = jax.scipy.linalg.solve_triangular(
        unit_lower, value_block, lower=True, unit_diagonal=True
    )
    solved_keys = jax.scipy.linalg.solve_triangular(
        unit_lower, key_grown, lower=True, unit_diagonal=True
    )
    query_mix = (
        jnp.einsum("...id,...jd->...ij", query_grown, key_shrunk, precision=exact_precision)
        * with_diagonal
        * weight_row
    )
    end_keys = key_shrunk * end_decay * strength[..., :, None]
    return (solved_values, solved_keys, query_grown, query_mix, end_keys, end_decay)


def advance(running_state, prepared):
    solved_values, solved_keys, query_grown, query_mix, end_keys, end_decay = prepared
    written = solved_values - jnp.einsum(
        "hcd,hde->hce", solved_keys, running_state, precision=exact_precision
    )
    core_out = jnp.einsum("hcd,hde->hce", query_grown, running_state, precision=exact_precision)
    core_out = core_out + jnp.einsum("hij,hje->hie", query_mix, written, precision=exact_precision)
    running_state = end_decay[:, 0, :, None] * running_state + jnp.einsum(
        "hcd,hce->hde", end_keys, written, precision=exact_precision
    )
    return (running_state, core_out)


def combine(earlier, later):
    joined_map = jnp.einsum("hde,hef->hdf", later[0], earlier[0], precision=exact_precision)
    joined_offset = (
        jnp.einsum("hde,hef->hdf", later[0], earlier[1], precision=exact_precision) + later[1]
    )
    return (joined_map, joined_offset)


def per_device(
    queries, key_vectors, value_vectors, log_decay, write_strength, out_gain, out_weight
):
    tok_rows = queries.shape[1]
    heads_here = write_strength.shape[1]
    head_size = queries.shape[2] // heads_here
    group_count = tok_rows // GROUP

    def to_heads(values):
        return (
            values[0]
            .astype(jnp.float32)
            .reshape(group_count, GROUP, heads_here, head_size)
            .transpose(0, 2, 1, 3)
        )

    query_block = to_heads(queries)
    key_unit = unit_rows(to_heads(key_vectors))
    value_block = to_heads(value_vectors)
    decay_block = to_heads(log_decay)
    strength = write_strength[0].reshape(heads_here, group_count, GROUP).transpose(1, 0, 2)
    prepared = prepare(query_block, key_unit, value_block, decay_block, strength)
    solved_values, solved_keys, query_grown, query_mix, end_keys, end_decay = prepared
    identity_matrix = jnp.broadcast_to(
        jnp.eye(head_size, dtype=jnp.float32), (heads_here, head_size, head_size)
    )
    zero_offset = jnp.zeros((heads_here, head_size, head_size), jnp.float32)
    group_maps = identity_matrix[None] * end_decay[..., 0, :, None] - jnp.einsum(
        "nhcd,nhce->nhde", end_keys, solved_keys, precision=exact_precision
    )
    group_offsets = jnp.einsum(
        "nhcd,nhce->nhde", end_keys, solved_values, precision=exact_precision
    )

    def compose(running, pieces):
        return (combine(running, pieces), running)

    (total_map, total_offset), (map_before, offset_before) = lax.scan(
        compose, (identity_matrix, zero_offset), (group_maps, group_offsets)
    )
    prefix = prefix_2((total_map, total_offset), "seq", combine, (identity_matrix, zero_offset))
    start_state = prefix[1]
    _, core_all = lax.scan(advance, start_state, prepared)
    core_rows = core_all.transpose(0, 2, 1, 3).reshape(tok_rows, heads_here, head_size)
    inverse_rms = lax.rsqrt(jnp.mean(core_rows * core_rows, axis=-1, keepdims=True) + 1e-05)
    normed = (
        (core_rows * inverse_rms * out_gain[0].reshape(heads_here, head_size))
        .reshape(tok_rows, heads_here * head_size)
        .astype(jnp.bfloat16)
    )
    mixer = jnp.dot(
        normed,
        lax.all_gather(out_weight[0], "seq", axis=1, tiled=True),
        preferred_element_type=jnp.float32,
    ).astype(jnp.bfloat16)
    return shifted(mixer[None], "section", 1)


def solution(mesh):
    in_specs = (
        P("section", "seq", None),
        P("section", "seq", None),
        P("section", "seq", None),
        P("section", "seq", None),
        P("section", None, "seq"),
        P("section", None),
        P("section", None, "seq"),
    )
    out_specs = P("section", "seq", None)
    return jax.shard_map(
        per_device, mesh=mesh, in_specs=in_specs, out_specs=out_specs, check_vma=False
    )
```

profile of v0, /device:TPU:0, one launch (start us, length us, event | category | flops | bytes accessed | tf_op | source)
XLA Modules:
  0.0 632.4 jit_solution(4477858384680547893)
XLA Ops:
  8.8 13.4 %fusion.78 = (f32[2,16,64,128]{3,1,2,0:T(8,128)S(1)}, f32[2,16,64,128]{3,1,2,0:T(8,128)S(1)}) fusion(f32[2,64,16,128]{3,2,1,0:T(8,128)S(1)} %bitcast.188), kind=kOutput, calls=%fused_computation.104 | output fusion | flops 16515072 | bytes 3145728 | tf_op jit(solution)/shard_map/jit(cumsum)/reduce_window_sum | solution.py:41
  26.2 2.3 fusion.47
  28.5 158.0 %custom-call.6 = f32[2,16,1,64,64]{3,4,2,1,0:T(8,128)} custom-call(f32[2,16,1,64,64]{4,3,2,1,0:T(8,128)S(1)} %fusion.47), custom_call_target="InvertDiagBlocksLowerTriangular" | custom-call | tf_op jit(solution)/shard_map/jit(_solve_triangular)/vmap(vmap())/triangular_solve | solution.py:62
  186.5 3.3 fusion.58
  194.4 4.8 fusion.74
  199.3 5.4 multiply_subtract_fusion
  204.8 10.6 %while.40 = (s32[]{:T(128)}, f32[16,128,128]{2,1,0:T(8,128)S(1)}, f32[16,128,128]{2,1,0:T(8,128)}, f32[2,16,128,128]{3,2,1,0:T(8,128)S(1)}, f32[2,16,128,128]{3,2,1,0:T(8,128)}, /*index=5*/s32[]{:T(128)}, s32[]{:T(128)}) while((s32[]{:T(128)}, f32[16,128,128]{2,1,0:T(8,128)S(1)}, f32[16,128,128]{2,1,0:T(8,128)}, ...), condition=%wide.region_3.5_spmd.clone, body=%wide.region_2.4_spmd.clone.sunk | while | flops 805830656 | bytes 19924088 | solution.py:132
  219.3 2.6 copy.69
  221.9 3.3 fusion.42
  225.2 119.0 %all-gather.7.cloned.1.call-done = f32[128,128,128]{2,1,0:T(8,128)} async-done(((f32[16,128,128]{2,1,0:T(8,128)}), f32[128,128,128]{2,1,0:T(8,128)}) %all-gather.7.cloned.1.call-update) | async-done | bytes 8388624 | tf_op jit(solution)/shard_map/all_gather | solution.py:14
  344.2 125.3 %all-gather.9.cloned.1.call-done = f32[128,128,128]{2,1,0:T(8,128)} async-done(((f32[16,128,128]{2,1,0:T(8,128)}), f32[128,128,128]{2,1,0:T(8,128)}) %all-gather.9.cloned.1.call-update) | async-done | bytes 8388624 | tf_op jit(solution)/shard_map/all_gather | solution.py:14
  469.5 23.9 %while.41 = (s32[]{:T(128)}, f32[16,128,128]{2,1,0:T(8,128)S(1)}, s32[]{:T(128)}, f32[8,16,128,128]{3,2,1,0:T(8,128)}, f32[8,16,128,128]{3,2,1,0:T(8,128)}, /*index=5*/s32[]{:T(128)}, s32[]{:T(128)}) while((s32[]{:T(128)}, f32[16,128,128]{2,1,0:T(8,128)S(1)}, s32[]{:T(128)}, f32[8,16,128,128]{3,2,1,0:T(8,128)}, ...), condition=%wide.region_5.7_spmd.clone, body=%wide.region_4.6_spmd.clone.sunk | while | flops 403701760 | bytes 7342687 | solution.py:26
  469.6 3.0 fusion.121
  472.7 2.8 fusion.121
  475.6 3.0 fusion.121
  478.7 2.9 fusion.121
  481.7 2.8 fusion.121
  484.7 2.8 fusion.121
  487.6 2.8 fusion.121
  490.6 2.8 fusion.121
  493.4 12.5 %while.39 = (s32[]{:T(128)}, f32[16,128,128]{2,1,0:T(8,128)S(1)}, f32[2,16,64,128]{3,2,1,0:T(8,128)}, f32[2,16,1,128]{3,1,2,0:T(8,128)S(1)}, f32[2,16,64,128]{3,...) while((s32[]{:T(128)}, f32[16,128,128]{2,1,0:T(8,128)S(1)}, ...), condition=%wide.region_7.9_spmd, body=%wide.region_6.8_spmd.sunk | while | flops 705429504 | bytes 28862716 | solution.py:137
  509.5 98.5 %all-gather.11.cloned.1.call-done = bf16[1,2048,2304]{1,2,0:T(8,128)(2,1)} async-done(((bf16[1,2048,288]{1,2,0:T(8,128)(2,1)}), bf16[1,2048,2304]{1,2,0:T(8,128)(2,1)}) %all-gather.11.cloned.1.call-update) | async-done | bytes 9437200 | tf_op jit(solution)/shard_map/all_gather | solution.py:147
  608.3 7.4 %fusion.39 = bf16[1,128,2304]{2,1,0:T(8,128)(2,1)S(1)} fusion(bf16[1,2048,2304]{1,2,0:T(8,128)(2,1)} %all-gather.11.cloned.1.call-done, f32[16,8,16,128]{3,2,1,0:T(8,128)S(1)} %bitcast.192, f32[16,8,16,128]{3,2,1,0:T(8,128)S(1)} %bitcast.191, f32[2048]{0:T(1024)S(1)} %bitcast.199), kind=kOutput, calls=%fused_computation.43 | convolution fusion | flops 1209040896 | bytes 12132352 | tf_op jit(solution)/shard_map/dot_general | solution.py:145
  615.8 9.3 %collective-permute-done = bf16[1,128,2304]{2,1,0:T(8,128)(2,1)S(1)} collective-permute-done((bf16[1,128,2304]{2,1,0:T(8,128)(2,1)S(1)}, bf16[1,128,2304]{2,1,0:T(8,128)(2,1)S(1)}, u32[]{:S(2)}, u32[]{:S(2)}) %collective-permute-start) | collective-permute-done | bytes 589856 | tf_op jit(solution)/shard_map/ppermute | solution.py:32
  (119 shorter events, 42.7 us)
Async XLA Ops:
  6.5 337.7 %all-gather.7.cloned.1.call-start = ((), (), s32[]{:S(2)}) async-start(), calls=%async_computation | async-start | bytes 9437184 | tf_op jit(solution)/shard_map/all_gather | solution.py:14
  8.8 13.5 %copy-start.17 = (bf16[1,128,2048]{2,1,0:T(8,128)(2,1)S(1)}, bf16[1,128,2048]{2,1,0:T(8,128)(2,1)}, u32[]{:S(2)}) copy-start(bf16[1,128,2048]{2,1,0:T(8,128)(2,1)} %param.16) | copy-start | bytes 1572868
  25.2 168.3 %copy-start.6 = (f32[2,16,64,128]{3,1,2,0:T(8,128)}, f32[2,16,64,128]{3,1,2,0:T(8,128)S(1)}, u32[]{:S(2)}) copy-start(f32[2,16,64,128]{3,1,2,0:T(8,128)S(1)} %get-tuple-element.289) | copy-start | bytes 3145732
  186.5 3.3 copy-start.19
  189.8 9.5 %copy-start.2 = (f32[2,16,64,128]{3,2,1,0:T(8,128)}, f32[2,16,64,128]{3,2,1,0:T(8,128)S(1)}, u32[]{:S(2)}) copy-start(f32[2,16,64,128]{3,2,1,0:T(8,128)S(1)} %fusion.58) | copy-start | bytes 3145732
  189.8 1.6 copy-start.14
  204.8 1.9 copy-start.1
  210.1 1.9 copy-start.1
  215.5 2.5 copy-start.7
  216.4 253.1 %all-gather.9.cloned.1.call-start = ((), (), s32[]{:S(2)}) async-start(), calls=%async_computation.1 | async-start | bytes 9437184 | tf_op jit(solution)/shard_map/all_gather | solution.py:14
  217.2 390.8 %all-gather.11.cloned.1.call-start = ((), (), s32[]{:S(2)}) async-start(), calls=%async_computation.2 | async-start | bytes 10616832 | tf_op jit(solution)/shard_map/all_gather | solution.py:147
  218.0 4.0 copy-start.12
  219.3 2.7 copy-start.13
  469.5 23.9 %copy-start.3 = (f32[2,16,64,128]{3,2,1,0:T(8,128)S(1)}, f32[2,16,64,128]{3,2,1,0:T(8,128)}, u32[]{:S(2)}) copy-start(f32[2,16,64,128]{3,2,1,0:T(8,128)} %copy-done.2) | copy-start | bytes 3145732
  469.5 23.9 %copy-start.5 = (f32[2,16,64,128]{3,2,1,0:T(8,128)S(1)}, f32[2,16,64,128]{3,2,1,0:T(8,128)}, u32[]{:S(2)}) copy-start(f32[2,16,64,128]{3,2,1,0:T(8,128)} %copy-done.4) | copy-start | bytes 3145732
  493.4 1.2 copy-start.9
  493.5 1.9 copy-start.8
  493.5 1.9 copy-start.15
  494.7 2.8 copy-start.10
  499.7 1.9 copy-start.8
  499.7 1.9 copy-start.15
  500.9 2.8 copy-start.10
  506.0 102.4 %copy-start.20 = (f32[1,2048]{1,0:T(1,128)S(1)}, f32[1,2048]{1,0:T(1,128)}, u32[]{:S(2)}) copy-start(f32[1,2048]{1,0:T(1,128)} %param.20) | copy-start | bytes 24580
  615.7 9.4 %collective-permute-start = (bf16[1,128,2304]{2,1,0:T(8,128)(2,1)S(1)}, bf16[1,128,2304]{2,1,0:T(8,128)(2,1)S(1)}, u32[]{:S(2)}, u32[]{:S(2)}) collective-permute-start(bf16[1,128,2304]{2,1,0:T(8,128)(2,1)S(1)} %fusion.39), channel_id=1, source_target_pairs={{0,1},{1,2},{2,3},{3,0},{4,5},{5,6},{6,7},{7,4},{8,9},{9,10},{10,1... | collective-permute-start | bytes 1769480 | tf_op jit(solution)/shard_map/ppermute | solution.py:32
  (7 other events, 7.3 us)
Sparse Core Ops, SparseCore 0:
  216.6 127.6 all-gather.6
  346.4 123.1 all-gather.8
  471.7 136.2 all-gather.10
where the time goes:
time: 633 us; the launch traced here: 632 us
  waiting for transfers between devices  353 us (56%)
  other arithmetic  176 us (28%)
  matrix products  68.2 us (11%)
  local copies, waits for them, and re-layouts  20.2 us (3%)
  between operations  13.5 us (2%)
    all_gather x2, waiting for transfers between devices, prefix_2(): everything = jax.tree.map(lambda part: lax.all_gather(part, axis), shard)  244 us
    another operation x3, other arithmetic, prepare(): jax.scipy.linalg.solve_triangular(unit_lower, key_grown, lower=True, unit...  158 us
    all_gather x1, waiting for transfers between devices, per_device(): lax.all_gather(out_weight[0], 'seq', axis=1, tiled=True)  98.5 us
    dot_general x10, matrix products, combine(): jnp.einsum('hde,hef->hdf', later[0], earlier[1], precision=exact_precision)  27.3 us
    another operation x1, other arithmetic, prepare(): cumulative = jnp.cumsum(decay_block, axis=-2)  13.4 us
  transfers between devices with their start and end apart: 4, of which 4 were waited for; matrix products, arithmetic and copies ran while one was open for 7% of the time, Pallas kernels for 0%

commit v1 on v0

v1 whole, which is shorter than its diff:
```python
import functools

import jax
import jax.numpy as jnp
from jax import lax
from jax.experimental import pallas as pl
from jax.experimental.pallas import tpu as pltpu
from jax.sharding import PartitionSpec as P

F32 = jnp.float32
BF16 = jnp.bfloat16
QUAD = 4
VMEM_LIMIT = 48 << 20


def split(a):
    high = a.astype(BF16)
    return high, (a - high.astype(F32)).astype(BF16)


def dot1(a, b, dims=((1,), (0,))):
    return lax.dot_general(a, b, (dims, ((), ())), preferred_element_type=F32)


def dot3(a, b, dims=((1,), (0,))):
    return dot1(a[0], b[0], dims) + dot1(a[0], b[1], dims) + dot1(a[1], b[0], dims)


ROWS = ((1,), (1,))


def iotas(n):
    row = lax.broadcasted_iota(jnp.int32, (n, n), 0)
    col = lax.broadcasted_iota(jnp.int32, (n, n), 1)
    return row, col


def unit_lower_inverse(strict, row, col):
    n = strict.shape[0]
    inverse = (row == col).astype(F32)
    size = 1
    while size < n:
        shift = size.bit_length() - 1
        joins = ((row >> (shift + 1)) == (col >> (shift + 1))) & ((row >> shift) > (col >> shift))
        below = jnp.where(joins, strict, 0.0)
        if size == 1:
            inverse = inverse - below
        else:
            parts = split(inverse)
            inverse = inverse - dot3(parts, split(dot3(split(below), parts)))
        size *= 2
    return inverse


def pick(pieces, rank):
    p = list(pieces)
    one = (rank & 1) == 1
    two = (rank & 2) == 2
    p = [jnp.where(one, p[x ^ 1], p[x]) for x in range(4)]
    return [jnp.where(two, p[x ^ 2], p[x]) for x in range(4)]


def pack_kl(rank_ref, k_ref, l_ref, b_ref, *outs):
    rank = rank_ref[0]
    tok = k_ref.shape[0]
    width = outs[0].shape[1]
    dk = 128
    heads = width // dk
    for x in range(4):
        owner = rank ^ x
        at = pl.multiple_of(owner * width, width)
        outs[x][0:tok, :] = k_ref[:, pl.ds(at, width)]
        outs[x][tok : 2 * tok, :] = l_ref[:, pl.ds(at, width)]
        for h in range(heads):
            strength = b_ref[pl.ds(owner * heads + h, 1), :]
            first, rest = split(strength)
            second, third = split(strength - first.astype(F32))
            rows = jnp.concatenate(
                [first.astype(F32), second.astype(F32), third.astype(F32), jnp.zeros((13, tok), F32)], axis=0
            )
            outs[x][2 * tok : 2 * tok + 16, h * dk : (h + 1) * dk] = rows.astype(BF16)


def pack_vq(rank_ref, v_ref, q_ref, *outs):
    rank = rank_ref[0]
    width = outs[0].shape[1]
    for x in range(4):
        at = pl.multiple_of((rank ^ x) * width, width)
        outs[x][...] = v_ref[:, pl.ds(at, width)]
        outs[4 + x][...] = q_ref[:, pl.ds(at, width)]


def decays(log_decay, row, col):
    cumulative = dot1((row >= col).astype(BF16), log_decay)
    n = cumulative.shape[0]
    middle = cumulative[n // 2 - 1 : n // 2, :]
    end = cumulative[n - 1 : n, :]
    return cumulative, middle, end


def states_kernel(rank_ref, *refs):
    kl = refs[0:4]
    v = refs[4:8]
    key_solved_ref, value_solved_ref, shrunk_ref, map_ref, state_ref, total_ref = refs[8:]
    rank = rank_ref[0]
    n = 128
    row, col = iotas(n)
    kl_c = pick([r[...] for r in kl], rank)
    v_c = pick([r[...] for r in v], rank)
    state = None
    for c in range(4):
        key = kl_c[c][0:n].astype(F32)
        log_decay = kl_c[c][n : 2 * n]
        bs = kl_c[c][2 * n : 2 * n + 16].astype(F32)
        strength = bs[0:1] + bs[1:2] + bs[2:3]
        strength_col = jnp.sum(jnp.where(row == col, strength, 0.0), axis=1, keepdims=True)
        key = key * lax.rsqrt(jnp.sum(key * key, axis=-1, keepdims=True) + 1e-06)
        cumulative, middle, end = decays(log_decay, row, col)
        grown = key * jnp.exp(cumulative - middle)
        shrunk = key * jnp.exp(middle - cumulative) * strength_col
        grown_s, shrunk_s = split(grown), split(shrunk)
        strict = jnp.where(row > col, dot3(grown_s, shrunk_s, ROWS), 0.0)
        inverse = split(unit_lower_inverse(strict, row, col))
        key_solved = dot3(inverse, grown_s) * jnp.exp(middle)
        value_solved = dot1(inverse[0], v_c[c]) + dot1(inverse[1], v_c[c])
        key_s, value_s = split(key_solved), split(value_solved)
        end_keys = split((shrunk * jnp.exp(end - middle)).T)
        end_col = jnp.sum(jnp.where(row == col, jnp.exp(end), 0.0), axis=1, keepdims=True)
        step = jnp.where(row == col, end_col, 0.0) - dot3(end_keys, key_s)
        offset = dot3(end_keys, value_s)
        key_solved_ref[0, c] = key_solved
        value_solved_ref[0, c] = value_solved
        shrunk_ref[0, c] = shrunk
        map_ref[0, c] = step
        if c == 0:
            state_ref[0, c] = jnp.zeros((n, n), F32)
            state = offset
        else:
            state_ref[0, c] = state
            state = dot3(split(step), split(state)) + offset
    total_ref[0] = state


def local_kernel(rank_ref, *refs):
    kl = refs[0:4]
    q = refs[4:8]
    key_solved_ref, value_solved_ref, shrunk_ref, state_ref, query_ref, core_ref = refs[8:]
    rank = rank_ref[0]
    n = 128
    row, col = iotas(n)
    l_c = pick([r[n : 2 * n] for r in kl], rank)
    q_c = pick([r[...] for r in q], rank)
    for c in range(4):
        cumulative, middle, end = decays(l_c[c], row, col)
        grown = q_c[c].astype(F32) * jnp.exp(cumulative - middle)
        mix = jnp.where(row >= col, dot3(split(grown), split(shrunk_ref[0, c]), ROWS), 0.0)
        mix_s = split(mix)
        query = grown * jnp.exp(middle) - dot3(mix_s, split(key_solved_ref[0, c]))
        core = dot3(mix_s, split(value_solved_ref[0, c]))
        if c > 0:
            core = core + dot3(split(query), split(state_ref[0, c]))
        query_ref[0, c] = query
        core_ref[0, c] = core


def finish_kernel(start_ref, map_ref, query_ref, core_ref, gain_ref, out_ref):
    state = start_ref[0].astype(F32)
    n = 128
    for c in range(4):
        state_s = split(state)
        core = core_ref[0, c] + dot3(split(query_ref[0, c]), state_s)
        if c < 3:
            state = dot3(split(map_ref[0, c]), state_s)
        scale = lax.rsqrt(jnp.mean(core * core, axis=-1, keepdims=True) + 1e-05)
        out_ref[c * n : (c + 1) * n, :] = (core * scale * gain_ref[...]).astype(BF16)


def per_device(q, k, v, l, strength, gain, weight):
    q, k, v, l, strength, gain, weight = (a[0] for a in (q, k, v, l, strength, gain, weight))
    tok, hk = q.shape
    heads = strength.shape[0]
    dk = hk // heads
    seq = lax.axis_size("seq")
    sections = lax.axis_size("section")
    groups = seq // QUAD
    width = hk // QUAD
    hq = heads // QUAD
    position = lax.axis_index("seq")
    rank = (position % QUAD).astype(jnp.int32)
    rank1 = rank.reshape(1)
    smem = pl.BlockSpec(memory_space=pltpu.SMEM)
    params = pltpu.CompilerParams(vmem_limit_bytes=VMEM_LIMIT)

    def call(kernel, name, **kw):
        return pl.pallas_call(kernel, name=name, compiler_params=params, **kw)

    def near(value, x):
        return lax.ppermute(value, "seq", [(i, i ^ x) for i in range(seq)])

    full = lambda shape: pl.BlockSpec(shape, lambda *_: (0,) * len(shape))
    kl = call(
        pack_kl,
        "pack_kl",
        grid=(1,),
        in_specs=[smem, full((tok, hk)), full((tok, hk)), full((heads, tok))],
        out_specs=[full((2 * tok + 16, width))] * 4,
        out_shape=[jax.ShapeDtypeStruct((2 * tok + 16, width), BF16)] * 4,
    )(rank1, k, l, strength)
    vq = call(
        pack_vq,
        "pack_vq",
        grid=(1,),
        in_specs=[smem, full((tok, hk)), full((tok, hk))],
        out_specs=[full((tok, width))] * 8,
        out_shape=[jax.ShapeDtypeStruct((tok, width), BF16)] * 8,
    )(rank1, v, q)
    kl = [kl[0]] + [near(kl[x], x) for x in range(1, 4)]
    vs = [vq[0]] + [near(vq[x], x) for x in range(1, 4)]
    qs = [vq[4]] + [near(vq[4 + x], x) for x in range(1, 4)]
    far_weights = [weight]
    for g in range(1, groups):
        far_weights.append(
            lax.ppermute(weight, "seq", [(i, (i + g * QUAD) % seq) for i in range(seq)])
        )

    kl_spec = pl.BlockSpec((2 * tok + 16, dk), lambda h: (0, h))
    x_spec = pl.BlockSpec((tok, dk), lambda h: (0, h))
    m_spec = pl.BlockSpec((1, QUAD, tok, dk), lambda h: (h, 0, 0, 0))
    m_shape = jax.ShapeDtypeStruct((hq, QUAD, tok, dk), F32)
    s_spec = pl.BlockSpec((1, dk, dk), lambda h: (h, 0, 0))
    key_solved, value_solved, shrunk, maps, states, total = call(
        states_kernel,
        "states",
        grid=(hq,),
        in_specs=[smem] + [kl_spec] * 4 + [x_spec] * 4,
        out_specs=[m_spec] * 5 + [s_spec],
        out_shape=[m_shape] * 5 + [jax.ShapeDtypeStruct((hq, dk, dk), F32)],
    )(rank1, *kl, *vs)

    onward = [(i, i + QUAD) for i in range(seq - QUAD)]
    start = lax.ppermute(total, "seq", onward)
    for _ in range(groups - 2):
        state = start
        for c in range(QUAD):
            state = jnp.einsum("hde,hef->hdf", maps[:, c], state, precision=lax.Precision.HIGHEST)
        start = lax.ppermute(state + total, "seq", onward)

    query, core = call(
        local_kernel,
        "local",
        grid=(hq,),
        in_specs=[smem] + [kl_spec] * 4 + [x_spec] * 4 + [m_spec] * 4,
        out_specs=[m_spec] * 2,
        out_shape=[m_shape] * 2,
    )(rank1, *kl, *qs, key_solved, value_solved, shrunk, states)
    gain_here = lax.dynamic_slice(gain.reshape(QUAD, 1, width), (rank, 0, 0), (1, 1, width))[0]
    normed = call(
        finish_kernel,
        "finish",
        grid=(hq,),
        in_specs=[s_spec, m_spec, m_spec, m_spec, pl.BlockSpec((1, dk), lambda h: (0, h))],
        out_specs=pl.BlockSpec((QUAD * tok, dk), lambda h: (0, h)),
        out_shape=jax.ShapeDtypeStruct((QUAD * tok, width), BF16),
    )(start, maps, query, core, gain_here)

    normed = [normed] + [near(normed, x) for x in range(1, 4)]

    def product_kernel(rank_ref, *refs):
        n_refs, w_refs, outs = refs[:4], refs[4 : 4 + groups], refs[4 + groups :]
        rank = rank_ref[0]
        cols = weight.shape[1]
        parts = []
        for w in w_refs:
            acc = None
            for x in range(4):
                at = pl.multiple_of((rank ^ x) * width, width)
                term = dot1(n_refs[x][...], w[pl.ds(at, width), :])
                acc = term if acc is None else acc + term
            parts.append(acc.astype(BF16))
        for c in range(4):
            for g in range(groups):
                outs[c][:, g * cols : (g + 1) * cols] = parts[g][c * tok : (c + 1) * tok]

    cols = weight.shape[1]
    pieces = call(
        product_kernel,
        "product",
        grid=(1,),
        in_specs=[smem] + [full((QUAD * tok, width))] * 4 + [full(weight.shape)] * groups,
        out_specs=[full((tok, groups * cols))] * 4,
        out_shape=[jax.ShapeDtypeStruct((tok, groups * cols), BF16)] * 4,
    )(rank1, *normed, *far_weights)

    sent = pick(pieces, rank)
    got = []
    for x in range(4):
        pairs = []
        for i in range(seq):
            for s in range(sections):
                pairs.append((i * sections + s, (i ^ x) * sections + (s + 1) % sections))
        got.append(lax.ppermute(sent[x], ("seq", "section"), pairs))
    by_rank = pick(got, rank)
    stack = jnp.stack(by_rank).reshape(QUAD, tok, groups, cols)
    group = position // QUAD
    columns = [
        lax.dynamic_index_in_dim(stack, (group - g) % groups, axis=2, keepdims=False)
        for g in range(groups)
    ]
    out = jnp.stack(columns)
    out = out.transpose(2, 0, 1, 3).reshape(tok, groups * QUAD * cols)
    return out[None]


def solution(mesh):
    in_specs = (
        P("section", "seq", None),
        P("section", "seq", None),
        P("section", "seq", None),
        P("section", "seq", None),
        P("section", None, "seq"),
        P("section", None),
        P("section", None, "seq"),
    )
    out_specs = P("section", "seq", None)
    return jax.shard_map(
        per_device, mesh=mesh, in_specs=in_specs, out_specs=out_specs, check_vma=False
    )
```

time: 633 us -> 185 us (0.29)
  waiting for transfers between devices: 353 us -> 77.3 us
  other arithmetic: 176 us -> 0.98 us
  matrix products: 68.2 us -> 0 us
  Pallas kernels: 0 us -> 61.8 us
  starting transfers between devices: 0.14 us -> 28.9 us
  between operations: 13.5 us -> 0.16 us
    all_gather x3 -> x0, waiting for transfers between devices: 343 us -> none  [the longest x2 244 us: prefix_2(): everything = jax.tree.map(lambda part: lax.all_gather(part, axis), shard)]
    another operation x4 -> x2, other arithmetic: 171 us -> 0.14 us  [the longest x1 0.08 us: per_device(): stack = jnp.stack(by_rank).reshape(QUAD, tok, groups, cols)]
    ppermute x1 -> x18, waiting for transfers between devices: 9.29 us -> 77.3 us  [the longest x12 68.7 us: near(): return lax.ppermute(value, 'seq', [(i, i ^ x) for i in range(seq)])]
    dot_general x25 -> x0, matrix products: 62.8 us -> none  [the longest x10 27.3 us: combine(): jnp.einsum('hde,hef->hdf', later[0], earlier[1], precision=exact_precision)]
    pallas_call x0 -> x6, Pallas kernels: none -> 61.8 us  [the longest x1 45.7 us: per_device(): call(states_kernel, 'states', grid=(hq,), in_specs=[smem] + [kl_spec] * 4...]
    ppermute x1 -> x18, starting transfers between devices: 0.06 us -> 28.9 us  [the longest x12 18.5 us: near(): return lax.ppermute(value, 'seq', [(i, i ^ x) for i in range(seq)])]
    while x37 -> x0, local copies, waits for them, and re-layouts: 9.5 us -> none
  transfers between devices with their start and end apart: 4 -> 18, of which waited for: 4 -> 11; matrix products, arithmetic and copies ran while one was open for 7% -> 3% of each run, Pallas kernels for 0% -> 31%
where the time goes in v1:
time: 185 us
  waiting for transfers between devices  77.3 us (42%)
  Pallas kernels  61.8 us (33%)
  starting transfers between devices  28.9 us (16%)
  local copies, waits for them, and re-layouts  15.6 us (8%)
    ppermute x12, waiting for transfers between devices, near(): return lax.ppermute(value, 'seq', [(i, i ^ x) for i in range(seq)])  68.7 us
    pallas_call x1, Pallas kernels, per_device(): call(states_kernel, 'states', grid=(hq,), in_specs=[smem] + [kl_spec] * 4...  45.7 us
    ppermute x12, starting transfers between devices, near(): return lax.ppermute(value, 'seq', [(i, i ^ x) for i in range(seq)])  18.5 us
    unnamed x24, local copies, waits for them, and re-layouts  12 us
    ppermute x4, waiting for transfers between devices, per_device(): got.append(lax.ppermute(sent[x], ('seq', 'section'), pairs))  8.52 us
    pallas_call x1, Pallas kernels, per_device(): call(local_kernel, 'local', grid=(hq,), in_specs=[smem] + [kl_spec] * 4 +...  7.16 us
    ppermute x4, starting transfers between devices, per_device(): got.append(lax.ppermute(sent[x], ('seq', 'section'), pairs))  4.27 us
    pallas_call x1, Pallas kernels, per_device(): call(finish_kernel, 'finish', grid=(hq,), in_specs=[s_spec, m_spec, m_spe...  4.17 us
  transfers between devices with their start and end apart: 18, of which 11 were waited for; matrix products, arithmetic and copies ran while one was open for 3% of the time, Pallas kernels for 31%

profile of v1, /device:TPU:0, one launch (start us, length us, event | category | flops | bytes accessed | tf_op | source)
XLA Modules:
  0.0 184.7 jit_solution(7191816749426895251)
XLA Ops:
  3.5 3.0 %collective-permute-start.3 = (bf16[128,512]{1,0:T(8,128)(2,1)S(1)}, bf16[128,512]{1,0:T(8,128)(2,1)S(1)}, u32[]{:S(2)}, u32[]{:S(2)}) collective-permute-start(bf16[128,512]{1,0:T(8,128)(2,1)S(1)} %get-tuple-element.34), channel_id=1, source_target_pairs={{0,4},{4,0},{8,12},{12,8},{16,20},{20,16},{24,28},{28,24},{1,5},{5... | collective-permute-start | bytes 393224 | tf_op jit(solution)/shard_map/ppermute | solution.py:198
  6.5 2.6 %collective-permute-start.13 = (bf16[2048,288]{0,1:T(8,128)(2,1)}, bf16[2048,288]{0,1:T(8,128)(2,1)}, u32[]{:S(2)}, u32[]{:S(2)}) collective-permute-start(bf16[2048,288]{0,1:T(8,128)(2,1)} %bitcast.28), channel_id=1, source_target_pairs={{0,16},{4,20},{8,24},{12,28},{16,0},{20,4},{24,8},{28,12},{1,17},{... | collective-permute-start | bytes 3538952 | tf_op jit(solution)/shard_map/ppermute | solution.py:223
  12.5 1.6 collective-permute-start.1
  15.5 1.6 collective-permute-start.4
  17.1 31.9 %collective-permute-done.4.refs_6_ = bf16[128,512]{1,0:T(8,128)(2,1)S(1)} collective-permute-done((bf16[128,512]{1,0:T(8,128)(2,1)S(1)}, bf16[128,512]{1,0:T(8,128)(2,1)S(1)}, u32[]{:S(2)}, u32[]{:S(2)}) %collective-permute-start.4) | collective-permute-done | bytes 131104 | tf_op jit(solution)/shard_map/ppermute | solution.py:198
  49.0 2.4 %collective-permute-start.5 = (bf16[128,512]{1,0:T(8,128)(2,1)S(1)}, bf16[128,512]{1,0:T(8,128)(2,1)S(1)}, u32[]{:S(2)}, u32[]{:S(2)}) collective-permute-start(bf16[128,512]{1,0:T(8,128)(2,1)S(1)} %get-tuple-element.36), channel_id=1, source_target_pairs={{0,12},{4,8},{8,4},{12,0},{16,28},{20,24},{24,20},{28,16},{1,13},{... | collective-permute-start | bytes 393224 | tf_op jit(solution)/shard_map/ppermute | solution.py:198
  51.4 11.6 %collective-permute-done.5.refs_7_ = bf16[128,512]{1,0:T(8,128)(2,1)S(1)} collective-permute-done((bf16[128,512]{1,0:T(8,128)(2,1)S(1)}, bf16[128,512]{1,0:T(8,128)(2,1)S(1)}, u32[]{:S(2)}, u32[]{:S(2)}) %collective-permute-start.5) | collective-permute-done | bytes 131104 | tf_op jit(solution)/shard_map/ppermute | solution.py:198
  63.0 45.7 %states.1 = (f32[4,4,128,128]{3,2,1,0:T(8,128)S(1)}, f32[4,4,128,128]{3,2,1,0:T(8,128)S(1)}, f32[4,4,128,128]{3,2,1,0:T(8,128)S(1)}, f32[4,4,128,128]{3,2,1,0:T(...) custom-call(s32[1]{0:T(128)} %bitcast.rank_ref, bf16[272,512]{1,0:T(8,128)(2,1)S(1)} %get-tuple-element.29.refs_0_, ...), custom_call_target="tpu_custom_call" | custom-call | tf_op jit(solution)/shard_map/states/pallas_call | solution.py:231
  110.7 3.6 %collective-permute-start.6 = (f32[4,128,128]{2,1,0:T(8,128)}, f32[4,128,128]{2,1,0:T(8,128)S(1)}, u32[]{:S(2)}, u32[]{:S(2)}) collective-permute-start(f32[4,128,128]{2,1,0:T(8,128)} %get-tuple-element.37), channel_id=1, source_target_pairs={{0,16},{4,20},{8,24},{12,28},{1,17},{5,21},{9,25},{13,29},{2,18},{... | collective-permute-start | bytes 786440 | tf_op jit(solution)/shard_map/ppermute | solution.py:241
  114.9 3.4 %collective-permute-start.8 = (bf16[128,512]{1,0:T(8,128)(2,1)}, bf16[128,512]{1,0:T(8,128)(2,1)}, u32[]{:S(2)}, u32[]{:S(2)}) collective-permute-start(bf16[128,512]{1,0:T(8,128)(2,1)} %get-tuple-element.41), channel_id=1, source_target_pairs={{0,8},{4,12},{8,0},{12,4},{16,24},{20,28},{24,16},{28,20},{1,9},{5... | collective-permute-start | bytes 393224 | tf_op jit(solution)/shard_map/ppermute | solution.py:198
  119.8 4.3 %collective-permute-done.8.refs_6_ = bf16[128,512]{1,0:T(8,128)(2,1)} collective-permute-done((bf16[128,512]{1,0:T(8,128)(2,1)}, bf16[128,512]{1,0:T(8,128)(2,1)}, u32[]{:S(2)}, u32[]{:S(2)}) %collective-permute-start.8) | collective-permute-done | bytes 131104 | tf_op jit(solution)/shard_map/ppermute | solution.py:198
  124.1 1.9 %collective-permute-done.9.refs_7_ = bf16[128,512]{1,0:T(8,128)(2,1)} collective-permute-done((bf16[128,512]{1,0:T(8,128)(2,1)}, bf16[128,512]{1,0:T(8,128)(2,1)}, u32[]{:S(2)}, u32[]{:S(2)}) %collective-permute-start.9) | collective-permute-done | bytes 131104 | tf_op jit(solution)/shard_map/ppermute | solution.py:198
  128.1 7.2 %local.1 = (f32[4,4,128,128]{3,2,1,0:T(8,128)S(1)}, f32[4,4,128,128]{3,2,1,0:T(8,128)S(1)}) custom-call(s32[1]{0:T(128)} %bitcast.rank_ref, bf16[272,512]{1,0:T(8,128)(2,1)S(1)} %get-tuple-element.29.refs_0_, bf16[272,512]{1,0:T(8,128)(2,1)S(1)} %collective-permute-done.refs_1_, bf16[272,512]{1,0:T(8,128)(2,1)S(1)} %collective-permute-done.1.refs_2_, ...), custom_call_target="tpu_custom_call" | custom-call | tf_op jit(solution)/shard_map/local/pallas_call | solution.py:248
  135.3 4.2 %finish.1.refs_0_ = bf16[512,512]{1,0:T(8,128)(2,1)} custom-call(f32[4,128,128]{2,1,0:T(8,128)S(1)} %collective-permute-done.6.start_ref, f32[4,4,128,128]{3,2,1,0:T(8,128)S(1)} %get-tuple-element.38.map_ref, f32[4,4,128,128]{3,2,1,0:T(8,128)S(1)} %get-tuple-element.47.query_ref, f32[4,4,128,128]{3,2,1,0:T(8,128)S(1)} %get-tuple-element.48.core_ref, ...), custom_call_target="tpu_custom_call" | custom-call | tf_op jit(solution)/shard_map/finish/pallas_call | solution.py:257
  140.0 3.4 %collective-permute-start.11 = (bf16[512,512]{1,0:T(8,128)(2,1)}, bf16[512,512]{1,0:T(8,128)(2,1)}, u32[]{:S(2)}, u32[]{:S(2)}) collective-permute-start(bf16[512,512]{1,0:T(8,128)(2,1)} %finish.1.refs_0_), channel_id=1, source_target_pairs={{0,8},{4,12},{8,0},{12,4},{16,24},{20,28},{24,16},{28,20},{1,9},{5... | collective-permute-start | bytes 1572872 | tf_op jit(solution)/shard_map/ppermute | solution.py:198
  143.4 1.8 copy.15
  145.3 1.8 copy.17.refs_5_
  147.1 5.7 %collective-permute-done.10.refs_1_ = bf16[512,512]{1,0:T(8,128)(2,1)} collective-permute-done((bf16[512,512]{1,0:T(8,128)(2,1)}, bf16[512,512]{1,0:T(8,128)(2,1)}, u32[]{:S(2)}, u32[]{:S(2)}) %collective-permute-start.10) | collective-permute-done | bytes 524320 | tf_op jit(solution)/shard_map/ppermute | solution.py:198
  152.8 3.8 %collective-permute-done.11.refs_2_ = bf16[512,512]{1,0:T(8,128)(2,1)} collective-permute-done((bf16[512,512]{1,0:T(8,128)(2,1)}, bf16[512,512]{1,0:T(8,128)(2,1)}, u32[]{:S(2)}, u32[]{:S(2)}) %collective-permute-start.11) | collective-permute-done | bytes 524320 | tf_op jit(solution)/shard_map/ppermute | solution.py:198
  156.6 9.3 %collective-permute-done.12.refs_3_ = bf16[512,512]{1,0:T(8,128)(2,1)} collective-permute-done((bf16[512,512]{1,0:T(8,128)(2,1)}, bf16[512,512]{1,0:T(8,128)(2,1)}, u32[]{:S(2)}, u32[]{:S(2)}) %collective-permute-start.12) | collective-permute-done | bytes 524320 | tf_op jit(solution)/shard_map/ppermute | solution.py:198
  165.9 3.9 %product.1 = (bf16[128,576]{1,0:T(8,128)(2,1)S(1)}, bf16[128,576]{1,0:T(8,128)(2,1)S(1)}, bf16[128,576]{1,0:T(8,128)(2,1)S(1)}, bf16[128,576]{1,0:T(8,128)(2,1)S(1)}) custom-call(s32[1]{0:T(128)} %bitcast.rank_ref, bf16[512,512]{1,0:T(8,128)(2,1)} %finish.1.refs_0_, bf16[512,512]{1,0:T(8,128)(2,1)} %collective-permute-done.10.refs_1_, ...), custom_call_target="tpu_custom_call" | custom-call | tf_op jit(solution)/shard_map/product/pallas_call | solution.py:285
  170.3 3.4 %collective-permute-start.15 = (bf16[128,576]{1,0:T(8,128)(2,1)S(1)}, bf16[128,576]{1,0:T(8,128)(2,1)S(1)}, u32[]{:S(2)}, u32[]{:S(2)}) collective-permute-start(bf16[128,576]{1,0:T(8,128)(2,1)S(1)} %get-tuple-element.58), channel_id=1, source_target_pairs={{0,9},{1,10},{2,11},{3,8},{4,13},{5,14},{6,15},{7,12},{8,1},{9,2},... | collective-permute-start | bytes 442376 | tf_op jit(solution)/shard_map/ppermute | solution.py:301
  174.2 3.8 %collective-permute-done.14 = bf16[128,576]{1,0:T(8,128)(2,1)S(1)} collective-permute-done((bf16[128,576]{1,0:T(8,128)(2,1)S(1)}, bf16[128,576]{1,0:T(8,128)(2,1)S(1)}, u32[]{:S(2)}, u32[]{:S(2)}) %collective-permute-start.14) | collective-permute-done | bytes 147488 | tf_op jit(solution)/shard_map/ppermute | solution.py:301
  178.1 3.2 %collective-permute-done.15 = bf16[128,576]{1,0:T(8,128)(2,1)S(1)} collective-permute-done((bf16[128,576]{1,0:T(8,128)(2,1)S(1)}, bf16[128,576]{1,0:T(8,128)(2,1)S(1)}, u32[]{:S(2)}, u32[]{:S(2)}) %collective-permute-start.15) | collective-permute-done | bytes 147488 | tf_op jit(solution)/shard_map/ppermute | solution.py:301
  (56 shorter events, 19.5 us)
Async XLA Ops:
  0.0 1.0 copy-start.3
  1.0 1.0 copy-start.4
  3.5 115.4 %copy-start.10 = (f32[1,2048]{1,0:T(1,128)S(1)}, f32[1,2048]{1,0:T(1,128)}, u32[]{:S(2)}) copy-start(f32[1,2048]{1,0:T(1,128)} %param.12) | copy-start | bytes 24580
  3.5 12.0 %collective-permute-start.3 = (bf16[128,512]{1,0:T(8,128)(2,1)S(1)}, bf16[128,512]{1,0:T(8,128)(2,1)S(1)}, u32[]{:S(2)}, u32[]{:S(2)}) collective-permute-start(bf16[128,512]{1,0:T(8,128)(2,1)S(1)} %get-tuple-element.34), channel_id=1, source_target_pairs={{0,4},{4,0},{8,12},{12,8},{16,20},{20,16},{24,28},{28,24},{1,5},{5... | collective-permute-start | bytes 393224 | tf_op jit(solution)/shard_map/ppermute | solution.py:198
  6.5 138.8 %collective-permute-start.13 = (bf16[2048,288]{0,1:T(8,128)(2,1)}, bf16[2048,288]{0,1:T(8,128)(2,1)}, u32[]{:S(2)}, u32[]{:S(2)}) collective-permute-start(bf16[2048,288]{0,1:T(8,128)(2,1)} %bitcast.28), channel_id=1, source_target_pairs={{0,16},{4,20},{8,24},{12,28},{16,0},{20,4},{24,8},{28,12},{1,17},{... | collective-permute-start | bytes 3538952 | tf_op jit(solution)/shard_map/ppermute | solution.py:223
  9.1 1.0 copy-start.5
  10.1 1.0 copy-start.6
  12.0 51.1 %collective-permute-start = (bf16[272,512]{1,0:T(8,128)(2,1)S(1)}, bf16[272,512]{1,0:T(8,128)(2,1)S(1)}, u32[]{:S(2)}, u32[]{:S(2)}) collective-permute-start(bf16[272,512]{1,0:T(8,128)(2,1)S(1)} %get-tuple-element.30), channel_id=1, source_target_pairs={{0,4},{4,0},{8,12},{12,8},{16,20},{20,16},{24,28},{28,24},{1,5},{5... | collective-permute-start | bytes 835592 | tf_op jit(solution)/shard_map/ppermute | solution.py:198
  12.5 50.5 %collective-permute-start.1 = (bf16[272,512]{1,0:T(8,128)(2,1)S(1)}, bf16[272,512]{1,0:T(8,128)(2,1)S(1)}, u32[]{:S(2)}, u32[]{:S(2)}) collective-permute-start(bf16[272,512]{1,0:T(8,128)(2,1)S(1)} %get-tuple-element.31), channel_id=1, source_target_pairs={{0,8},{4,12},{8,0},{12,4},{16,24},{20,28},{24,16},{28,20},{1,9},{5... | collective-permute-start | bytes 835592 | tf_op jit(solution)/shard_map/ppermute | solution.py:198
  14.1 48.9 %collective-permute-start.2 = (bf16[272,512]{1,0:T(8,128)(2,1)S(1)}, bf16[272,512]{1,0:T(8,128)(2,1)S(1)}, u32[]{:S(2)}, u32[]{:S(2)}) collective-permute-start(bf16[272,512]{1,0:T(8,128)(2,1)S(1)} %get-tuple-element.32), channel_id=1, source_target_pairs={{0,12},{4,8},{8,4},{12,0},{16,28},{20,24},{24,20},{28,16},{1,13},{... | collective-permute-start | bytes 835592 | tf_op jit(solution)/shard_map/ppermute | solution.py:198
  15.5 33.5 %collective-permute-start.4 = (bf16[128,512]{1,0:T(8,128)(2,1)S(1)}, bf16[128,512]{1,0:T(8,128)(2,1)S(1)}, u32[]{:S(2)}, u32[]{:S(2)}) collective-permute-start(bf16[128,512]{1,0:T(8,128)(2,1)S(1)} %get-tuple-element.35), channel_id=1, source_target_pairs={{0,8},{4,12},{8,0},{12,4},{16,24},{20,28},{24,16},{28,20},{1,9},{5... | collective-permute-start | bytes 393224 | tf_op jit(solution)/shard_map/ppermute | solution.py:198
  49.0 14.0 %collective-permute-start.5 = (bf16[128,512]{1,0:T(8,128)(2,1)S(1)}, bf16[128,512]{1,0:T(8,128)(2,1)S(1)}, u32[]{:S(2)}, u32[]{:S(2)}) collective-permute-start(bf16[128,512]{1,0:T(8,128)(2,1)S(1)} %get-tuple-element.36), channel_id=1, source_target_pairs={{0,12},{4,8},{8,4},{12,0},{16,28},{20,24},{24,20},{28,16},{1,13},{... | collective-permute-start | bytes 393224 | tf_op jit(solution)/shard_map/ppermute | solution.py:198
  110.7 24.6 %collective-permute-start.6 = (f32[4,128,128]{2,1,0:T(8,128)}, f32[4,128,128]{2,1,0:T(8,128)S(1)}, u32[]{:S(2)}, u32[]{:S(2)}) collective-permute-start(f32[4,128,128]{2,1,0:T(8,128)} %get-tuple-element.37), channel_id=1, source_target_pairs={{0,16},{4,20},{8,24},{12,28},{1,17},{5,21},{9,25},{13,29},{2,18},{... | collective-permute-start | bytes 786440 | tf_op jit(solution)/shard_map/ppermute | solution.py:241
  114.3 5.5 %collective-permute-start.7 = (bf16[128,512]{1,0:T(8,128)(2,1)}, bf16[128,512]{1,0:T(8,128)(2,1)}, u32[]{:S(2)}, u32[]{:S(2)}) collective-permute-start(bf16[128,512]{1,0:T(8,128)(2,1)} %get-tuple-element.40), channel_id=1, source_target_pairs={{0,4},{4,0},{8,12},{12,8},{16,20},{20,16},{24,28},{28,24},{1,5},{5... | collective-permute-start | bytes 393224 | tf_op jit(solution)/shard_map/ppermute | solution.py:198
  114.9 9.2 %collective-permute-start.8 = (bf16[128,512]{1,0:T(8,128)(2,1)}, bf16[128,512]{1,0:T(8,128)(2,1)}, u32[]{:S(2)}, u32[]{:S(2)}) collective-permute-start(bf16[128,512]{1,0:T(8,128)(2,1)} %get-tuple-element.41), channel_id=1, source_target_pairs={{0,8},{4,12},{8,0},{12,4},{16,24},{20,28},{24,16},{28,20},{1,9},{5... | collective-permute-start | bytes 393224 | tf_op jit(solution)/shard_map/ppermute | solution.py:198
  118.3 7.7 %collective-permute-start.9 = (bf16[128,512]{1,0:T(8,128)(2,1)}, bf16[128,512]{1,0:T(8,128)(2,1)}, u32[]{:S(2)}, u32[]{:S(2)}) collective-permute-start(bf16[128,512]{1,0:T(8,128)(2,1)} %get-tuple-element.42), channel_id=1, source_target_pairs={{0,12},{4,8},{8,4},{12,0},{16,28},{20,24},{24,20},{28,16},{1,13},{... | collective-permute-start | bytes 393224 | tf_op jit(solution)/shard_map/ppermute | solution.py:198
  126.0 1.2 copy-start.1
  139.5 13.3 %collective-permute-start.10 = (bf16[512,512]{1,0:T(8,128)(2,1)}, bf16[512,512]{1,0:T(8,128)(2,1)}, u32[]{:S(2)}, u32[]{:S(2)}) collective-permute-start(bf16[512,512]{1,0:T(8,128)(2,1)} %finish.1.refs_0_), channel_id=1, source_target_pairs={{0,4},{4,0},{8,12},{12,8},{16,20},{20,16},{24,28},{28,24},{1,5},{5... | collective-permute-start | bytes 1572872 | tf_op jit(solution)/shard_map/ppermute | solution.py:198
  140.0 16.6 %collective-permute-start.11 = (bf16[512,512]{1,0:T(8,128)(2,1)}, bf16[512,512]{1,0:T(8,128)(2,1)}, u32[]{:S(2)}, u32[]{:S(2)}) collective-permute-start(bf16[512,512]{1,0:T(8,128)(2,1)} %finish.1.refs_0_), channel_id=1, source_target_pairs={{0,8},{4,12},{8,0},{12,4},{16,24},{20,28},{24,16},{28,20},{1,9},{5... | collective-permute-start | bytes 1572872 | tf_op jit(solution)/shard_map/ppermute | solution.py:198
  143.4 22.5 %collective-permute-start.12 = (bf16[512,512]{1,0:T(8,128)(2,1)}, bf16[512,512]{1,0:T(8,128)(2,1)}, u32[]{:S(2)}, u32[]{:S(2)}) collective-permute-start(bf16[512,512]{1,0:T(8,128)(2,1)} %finish.1.refs_0_), channel_id=1, source_target_pairs={{0,12},{4,8},{8,4},{12,0},{16,28},{20,24},{24,20},{28,16},{1,13},{... | collective-permute-start | bytes 1572872 | tf_op jit(solution)/shard_map/ppermute | solution.py:198
  170.0 8.1 %collective-permute-start.14 = (bf16[128,576]{1,0:T(8,128)(2,1)S(1)}, bf16[128,576]{1,0:T(8,128)(2,1)S(1)}, u32[]{:S(2)}, u32[]{:S(2)}) collective-permute-start(bf16[128,576]{1,0:T(8,128)(2,1)S(1)} %get-tuple-element.60), channel_id=1, source_target_pairs={{0,13},{1,14},{2,15},{3,12},{4,9},{5,10},{6,11},{7,8},{8,5},{9,6},... | collective-permute-start | bytes 442376 | tf_op jit(solution)/shard_map/ppermute | solution.py:301
  170.3 11.0 %collective-permute-start.15 = (bf16[128,576]{1,0:T(8,128)(2,1)S(1)}, bf16[128,576]{1,0:T(8,128)(2,1)S(1)}, u32[]{:S(2)}, u32[]{:S(2)}) collective-permute-start(bf16[128,576]{1,0:T(8,128)(2,1)S(1)} %get-tuple-element.58), channel_id=1, source_target_pairs={{0,9},{1,10},{2,11},{3,8},{4,13},{5,14},{6,15},{7,12},{8,1},{9,2},... | collective-permute-start | bytes 442376 | tf_op jit(solution)/shard_map/ppermute | solution.py:301
  173.6 7.6 %collective-permute-start.16 = (bf16[128,576]{1,0:T(8,128)(2,1)S(1)}, bf16[128,576]{1,0:T(8,128)(2,1)S(1)}, u32[]{:S(2)}, u32[]{:S(2)}) collective-permute-start(bf16[128,576]{1,0:T(8,128)(2,1)S(1)} %get-tuple-element.57), channel_id=1, source_target_pairs={{0,5},{1,6},{2,7},{3,4},{4,1},{5,2},{6,3},{7,0},{8,13},{9,14},{10,... | collective-permute-start | bytes 442376 | tf_op jit(solution)/shard_map/ppermute | solution.py:301
  173.9 8.8 %collective-permute-start.17 = (bf16[128,576]{1,0:T(8,128)(2,1)S(1)}, bf16[128,576]{1,0:T(8,128)(2,1)S(1)}, u32[]{:S(2)}, u32[]{:S(2)}) collective-permute-start(bf16[128,576]{1,0:T(8,128)(2,1)S(1)} %get-tuple-element.59), channel_id=1, source_target_pairs={{0,1},{1,2},{2,3},{3,0},{4,5},{5,6},{6,7},{7,4},{8,9},{9,10},{10,1... | collective-permute-start | bytes 442376 | tf_op jit(solution)/shard_map/ppermute | solution.py:301
  (5 other events, 4.2 us)

commit v2 on v0

v2 whole, which is shorter than its diff:
```python
import functools

import jax
import jax.numpy as jnp
from jax import lax
from jax.experimental import pallas as pl
from jax.experimental.pallas import tpu as pltpu
from jax.sharding import PartitionSpec as P

F32 = jnp.float32
BF16 = jnp.bfloat16
QUAD = 4
SHARES = (8,)
ROWS = ((1,), (1,))


def split(a):
    high = a.astype(BF16)
    return high, (a - high.astype(F32)).astype(BF16)


def store_split(ref, at, a):
    high, low = split(a)
    n = a.shape[1]
    ref[(*at, slice(None), slice(0, n))] = high
    ref[(*at, slice(None), slice(n, 2 * n))] = low


def load_split(ref, at):
    both = ref[at]
    n = both.shape[1] // 2
    return both[:, :n], both[:, n:]


def dot1(a, b, dims=((1,), (0,))):
    return lax.dot_general(a, b, (dims, ((), ())), preferred_element_type=F32)


def dot2(a, b, dims=((1,), (0,))):
    return dot1(a[0], b, dims) + dot1(a[1], b, dims)


def dot3(a, b, dims=((1,), (0,))):
    return dot1(a[0], b[0], dims) + dot1(a[0], b[1], dims) + dot1(a[1], b[0], dims)


def iotas(n):
    row = lax.broadcasted_iota(jnp.int32, (n, n), 0)
    col = lax.broadcasted_iota(jnp.int32, (n, n), 1)
    return row, col


def unit_lower_inverses(stricts, row, col):
    n = stricts[0].shape[0]
    eye = (row == col).astype(F32)
    inverses = None
    size = 1
    while size < n:
        shift = size.bit_length() - 1
        joins = ((row >> (shift + 1)) == (col >> (shift + 1))) & ((row >> shift) > (col >> shift))
        below = [jnp.where(joins, s, 0.0) for s in stricts]
        if size == 1:
            inverses = [eye - b for b in below]
        else:
            parts = [split(i) for i in inverses]
            inner = [split(dot3(split(b), p)) for b, p in zip(below, parts)]
            outer = [dot3(p, t) for p, t in zip(parts, inner)]
            inverses = [i - o for i, o in zip(inverses, outer)]
        size *= 2
    return inverses


def pick(pieces, rank):
    p = list(pieces)
    one = (rank & 1) == 1
    two = (rank & 2) == 2
    p = [jnp.where(one, p[x ^ 1], p[x]) for x in range(4)]
    return [jnp.where(two, p[x ^ 2], p[x]) for x in range(4)]


def pack_kl(tok, width, dk, rank_ref, k_ref, l_ref, b_ref, *refs):
    outs, sem = refs[:4], refs[4]
    rank = rank_ref[0]
    heads = width // dk
    copies = []
    for x in range(4):
        at = pl.multiple_of((rank ^ x) * width, width)
        for i, source in enumerate((k_ref, l_ref)):
            copy = pltpu.make_async_copy(
                source.at[:, pl.ds(at, width)], outs[x].at[i * tok : (i + 1) * tok, :], sem.at[2 * x + i]
            )
            copy.start()
            copies.append(copy)
    for x in range(4):
        for h in range(heads):
            strength = b_ref[pl.ds((rank ^ x) * heads + h, 1), :]
            first, rest = split(strength)
            second, third = split(strength - first.astype(F32))
            rows = jnp.concatenate(
                [first.astype(F32), second.astype(F32), third.astype(F32), jnp.zeros((13, tok), F32)], axis=0
            )
            outs[x][2 * tok : 2 * tok + 16, h * dk : (h + 1) * dk] = rows.astype(BF16)
    for copy in copies:
        copy.wait()


def pack_vq(tok, width, rank_ref, v_ref, q_ref, *refs):
    outs, sem = refs[:4], refs[4]
    rank = rank_ref[0]
    copies = []
    for x in range(4):
        at = pl.multiple_of((rank ^ x) * width, width)
        for i, source in enumerate((v_ref, q_ref)):
            copy = pltpu.make_async_copy(
                source.at[:, pl.ds(at, width)], outs[x].at[i * tok : (i + 1) * tok, :], sem.at[2 * x + i]
            )
            copy.start()
            copies.append(copy)
    for copy in copies:
        copy.wait()


def chunks_of(refs, rank, rows, nh, dk):
    out = []
    for h in range(nh):
        out += pick([r[rows, h * dk : (h + 1) * dk] for r in refs], rank)
    return out


def maps_kernel(nh, n, more, rank_ref, *refs):
    kl = refs[0:4]
    inverse_ref, offset_ref, key_ref, shrunk_ref, map_ref, before_ref = refs[4:10]
    rank = rank_ref[0]
    row, col = iotas(n)
    diag = row == col
    tri = (row >= col).astype(BF16)
    every = range(4 * nh)
    at = [(i // 4, i % 4) for i in every]
    bs = [b.astype(F32) for b in chunks_of(kl, rank, slice(2 * n, 2 * n + 16), nh, n)]
    bs = [b[0:1] + b[1:2] + b[2:3] for b in bs]
    strength = [jnp.sum(jnp.where(diag, b, 0.0), axis=1, keepdims=True) for b in bs]
    key = [k.astype(F32) for k in chunks_of(kl, rank, slice(0, n), nh, n)]
    key = [k * lax.rsqrt(jnp.sum(k * k, axis=-1, keepdims=True) + 1e-06) for k in key]
    cum = [dot1(tri, l) for l in chunks_of(kl, rank, slice(n, 2 * n), nh, n)]
    mid = [c[n // 2 - 1 : n // 2] for c in cum]
    end = [c[n - 1 : n] for c in cum]
    grown = [split(key[i] * jnp.exp(cum[i] - mid[i])) for i in every]
    shrunk = [key[i] * jnp.exp(mid[i] - cum[i]) * strength[i] for i in every]
    shrunk_s = [split(s) for s in shrunk]
    strict = [jnp.where(row > col, dot3(grown[i], shrunk_s[i], ROWS), 0.0) for i in every]
    inverse = [split(x) for x in unit_lower_inverses(strict, row, col)]
    solved = [split(dot3(inverse[i], grown[i]) * jnp.exp(mid[i])) for i in every]
    end_keys = [split((shrunk[i] * jnp.exp(end[i] - mid[i])).T) for i in every]
    end_col = [jnp.sum(jnp.where(diag, jnp.exp(e), 0.0), axis=1, keepdims=True) for e in end]
    step = [jnp.where(diag, end_col[i], 0.0) - dot3(end_keys[i], solved[i]) for i in every]
    step_s = [split(s) for s in step]
    for i in every:
        for ref, value in ((inverse_ref, inverse[i]), (key_ref, solved[i]), (shrunk_ref, shrunk_s[i]), (map_ref, step_s[i])):
            ref[(*at[i], slice(None), slice(0, n))] = value[0]
            ref[(*at[i], slice(None), slice(n, 2 * n))] = value[1]
        store_split(offset_ref, at[i], dot3(end_keys[i], inverse[i]))
    before = [step[4 * h] for h in range(nh)]
    for c in range(1, 4):
        for h in range(nh):
            store_split(before_ref, (h, c - 1), before[h])
            if c < 3 or more:
                before[h] = dot3(step_s[4 * h + c], split(before[h]))
    if more:
        for h in range(nh):
            refs[10][h] = before[h]


def states_kernel(nh, n, rank_ref, *refs):
    v = refs[0:4]
    offset_ref, map_ref, state_ref, total_ref = refs[4:]
    value = chunks_of(v, rank_ref[0], slice(0, n), nh, n)
    offset = [dot2(load_split(offset_ref, (i // 4, i % 4)), value[i]) for i in range(4 * nh)]
    state = [offset[4 * h] for h in range(nh)]
    for c in range(1, 4):
        parts = [split(s) for s in state]
        for h in range(nh):
            state_ref[h, c - 1, :, 0:n] = parts[h][0]
            state_ref[h, c - 1, :, n : 2 * n] = parts[h][1]
        state = [dot3(load_split(map_ref, (h, c)), parts[h]) + offset[4 * h + c] for h in range(nh)]
    for h in range(nh):
        total_ref[h] = state[h].astype(total_ref.dtype)


def local_kernel(nh, n, rank_ref, *refs):
    kl, vq = refs[0:4], refs[4:8]
    inverse_ref, key_ref, shrunk_ref, before_ref, state_ref, query_ref, core_ref = refs[8:]
    rank = rank_ref[0]
    row, col = iotas(n)
    tri = (row >= col).astype(BF16)
    every = range(4 * nh)
    at = [(i // 4, i % 4) for i in every]
    value = chunks_of(vq, rank, slice(0, n), nh, n)
    query = [x.astype(F32) for x in chunks_of(vq, rank, slice(n, 2 * n), nh, n)]
    cum = [dot1(tri, l) for l in chunks_of(kl, rank, slice(n, 2 * n), nh, n)]
    mid = [c[n // 2 - 1 : n // 2] for c in cum]
    solved = [split(dot2(load_split(inverse_ref, at[i]), value[i])) for i in every]
    grown = [query[i] * jnp.exp(cum[i] - mid[i]) for i in every]
    mix = [
        split(jnp.where(row >= col, dot3(split(grown[i]), load_split(shrunk_ref, at[i]), ROWS), 0.0))
        for i in every
    ]
    query = [split(grown[i] * jnp.exp(mid[i]) - dot3(mix[i], load_split(key_ref, at[i]))) for i in every]
    core = [dot3(mix[i], solved[i]) for i in every]
    for i in every:
        h, c = at[i]
        if c == 0:
            core_ref[h, c] = core[i]
            query_ref[h, c, :, 0:n] = query[i][0]
            query_ref[h, c, :, n : 2 * n] = query[i][1]
        else:
            core_ref[h, c] = core[i] + dot3(query[i], load_split(state_ref, (h, c - 1)))
            store_split(query_ref, (h, c), dot3(query[i], load_split(before_ref, (h, c - 1))))


def finish_kernel(nh, n, rank_ref, start_ref, query_ref, core_ref, gain_ref, out_ref):
    for h in range(nh):
        start = start_ref[h]
        for c in range(4):
            core = core_ref[h, c] + dot2(load_split(query_ref, (h, c)), start)
            scale = lax.rsqrt(jnp.mean(core * core, axis=-1, keepdims=True) + 1e-05)
            gain = gain_ref[:, h * n : (h + 1) * n]
            out_ref[c * n : (c + 1) * n, h * n : (h + 1) * n] = (core * scale * gain).astype(BF16)


def product_kernel(offsets, width, n, rank_ref, *refs):
    normed, weights = refs[:4], refs[4 : 4 + len(offsets)]
    outs, scratch = refs[4 + len(offsets) : -1], refs[-1]
    rank = rank_ref[0]
    for w, offset in zip(weights, offsets):
        total = None
        for x in range(4):
            at = pl.multiple_of((rank ^ x) * width, width)
            term = dot1(w[:, pl.ds(at, width)], normed[x][...], ROWS)
            total = term if total is None else total + term
        scratch[offset : offset + w.shape[0], :] = total
    for x in range(4):
        at = pl.multiple_of((rank ^ x) * n, n)
        outs[x][...] = scratch[:, pl.ds(at, n)].astype(BF16)


def assemble_kernel(groups, cols, n, place_ref, *refs):
    pieces, out_ref, wide, tall = refs[:4], refs[4], refs[5], refs[6]
    rank, group = place_ref[0], place_ref[1]
    for x in range(4):
        wide[...] = pieces[x][...].astype(F32)
        for g in range(groups):
            there = lax.rem(group + groups - g, groups) * QUAD + (rank ^ x)
            at = pl.multiple_of(there * cols, 8)
            tall[pl.ds(at, cols), :] = wide[g * cols : (g + 1) * cols, :]
    for j in range(tall.shape[0] // n):
        out_ref[:, j * n : (j + 1) * n] = tall[j * n : (j + 1) * n, :].T.astype(BF16)


def per_device(q, k, v, l, strength, gain, weight):
    q, k, v, l, strength, weight = (a[0] for a in (q, k, v, l, strength, weight))
    tok, hk = q.shape
    heads = strength.shape[0]
    dk = hk // heads
    seq = lax.axis_size("seq")
    sections = lax.axis_size("section")
    groups = seq // QUAD
    width = hk // QUAD
    hq = heads // QUAD
    cols = weight.shape[1]
    position = lax.axis_index("seq")
    rank = (position & (QUAD - 1)).astype(jnp.int32)
    group = (position // QUAD).astype(jnp.int32)
    rank1 = rank.reshape(1)
    smem = pl.BlockSpec(memory_space=pltpu.SMEM)
    anywhere = pl.BlockSpec(memory_space=pltpu.HBM)

    def call(kernel, name, limit=16, **kw):
        params = pltpu.CompilerParams(vmem_limit_bytes=limit << 20)
        return pl.pallas_call(kernel, name=name, compiler_params=params, **kw)

    def shape(dims, dtype):
        return jax.ShapeDtypeStruct(dims, dtype)

    def in_hbm(value):
        return pltpu.with_memory_space_constraint(value, pltpu.HBM)

    def near(value, x):
        return lax.ppermute(value, "seq", [(i, i ^ x) for i in range(seq)])

    def full(dims):
        return pl.BlockSpec(dims, lambda *_: (0,) * len(dims))

    kl = call(
        functools.partial(pack_kl, tok, width, dk),
        "pack_kl",
        in_specs=[smem, anywhere, anywhere, pl.BlockSpec(memory_space=pltpu.VMEM)],
        out_shape=[shape((2 * tok + 16, width), BF16)] * 4,
        scratch_shapes=[pltpu.SemaphoreType.DMA((8,))],
    )(rank1, in_hbm(k), in_hbm(l), strength)
    vq = call(
        functools.partial(pack_vq, tok, width),
        "pack_vq",
        in_specs=[smem, anywhere, anywhere],
        out_shape=[shape((2 * tok, width), BF16)] * 4,
        scratch_shapes=[pltpu.SemaphoreType.DMA((8,))],
    )(rank1, in_hbm(v), in_hbm(q))
    kl = [kl[0]] + [near(kl[x], x) for x in range(1, 4)]
    weight = weight.T
    cuts = [0, *(cols * share // 24 // 8 * 8 for share in SHARES), cols]
    weights, offsets = [weight], [0]

    def send_part(i, *after):
        part, *_ = lax.optimization_barrier((weight[cuts[i] : cuts[i + 1]], *after))
        for g in range(1, groups):
            weights.append(lax.ppermute(part, "seq", [(j, (j + g * QUAD) % seq) for j in range(seq)]))
            offsets.append(g * cols + cuts[i])

    def wait_for(i, *values):
        at = slice(1 + i * (groups - 1), 1 + (i + 1) * (groups - 1))
        *values, parts = lax.optimization_barrier((*values, weights[at]))
        weights[at] = parts
        return values

    vq_1, vq_2, vq_3, *_ = lax.optimization_barrier((*vq[1:], kl[1], kl[2]))
    vq = [vq[0], near(vq_1, 1), near(vq_2, 2), near(vq_3, 3)]
    send_part(0, kl[1], kl[2])

    two = 2
    kl_spec = pl.BlockSpec((2 * tok + 16, two * dk), lambda h: (0, h))
    vq_spec = pl.BlockSpec((2 * tok, two * dk), lambda h: (0, h))
    v_spec = pl.BlockSpec((tok, hq * dk), lambda h: (0, h))
    pair = lambda count: pl.BlockSpec((two, count, tok, 2 * dk), lambda h: (h, 0, 0, 0))
    pairs = lambda count: shape((hq, count, tok, 2 * dk), BF16)
    more = groups > 2
    inverse, offset, key, shrunk, maps, before, *whole_map = call(
        functools.partial(maps_kernel, two, tok, more),
        "maps",
        limit=32,
        grid=(hq // two,),
        in_specs=[smem] + [kl_spec] * 4,
        out_specs=[pair(4)] * 5 + [pair(3)] + [pl.BlockSpec((two, dk, dk), lambda h: (h, 0, 0))] * more,
        out_shape=[pairs(4)] * 5 + [pairs(3)] + [shape((hq, dk, dk), F32)] * more,
    )(rank1, *kl)
    all4 = lambda count: full((hq, count, tok, 2 * dk))
    states, total = call(
        functools.partial(states_kernel, hq, tok),
        "states",
        limit=24,
        grid=(1,),
        in_specs=[smem] + [v_spec] * 4 + [all4(4)] * 2,
        out_specs=[all4(3), full((hq, dk, dk))],
        out_shape=[pairs(3), shape((hq, dk, dk), F32 if more else BF16)],
    )(rank1, *vq, offset, maps)

    onward = [(i, i + QUAD) for i in range(seq - QUAD)]
    start = lax.ppermute(total, "seq", onward)
    for _ in range(groups - 2):
        state = jnp.einsum("hde,hef->hdf", whole_map[0], start, precision=lax.Precision.HIGHEST)
        start = lax.ppermute(state + total, "seq", onward)
    start = start.astype(BF16)
    query, core = call(
        functools.partial(local_kernel, two, tok),
        "local",
        limit=32,
        grid=(hq // two,),
        in_specs=[smem] + [kl_spec] * 4 + [vq_spec] * 4 + [pair(4)] * 3 + [pair(3)] * 2,
        out_specs=[pair(4), pl.BlockSpec((two, 4, tok, dk), lambda h: (h, 0, 0, 0))],
        out_shape=[pairs(4), shape((hq, 4, tok, dk), F32)],
    )(rank1, *kl, *vq, inverse, key, shrunk, before, states)
    start, core = lax.optimization_barrier((start, core))
    start, core = wait_for(0, start, core)
    send_part(1, start)
    normed = call(
        functools.partial(finish_kernel, hq, tok),
        "finish",
        grid_spec=pltpu.PrefetchScalarGridSpec(
            num_scalar_prefetch=1,
            grid=(1,),
            in_specs=[
                full((hq, dk, dk)),
                all4(4),
                full((hq, 4, tok, dk)),
                pl.BlockSpec((1, width), lambda h, place: (0, place[0])),
            ],
            out_specs=full((QUAD * tok, width)),
        ),
        out_shape=shape((QUAD * tok, width), BF16),
    )(rank1, start, query, core, gain)

    beside, across = near(normed, 1), near(normed, 2)
    normed = [normed, beside, across, near(across, 1)]
    pieces = call(
        functools.partial(product_kernel, offsets, width, tok),
        "product",
        limit=24,
        grid=(1,),
        in_specs=[smem] + [full((QUAD * tok, width))] * 4 + [full(w.shape) for w in weights],
        out_specs=[full((groups * cols, tok))] * 4,
        out_shape=[shape((groups * cols, tok), BF16)] * 4,
        scratch_shapes=[pltpu.VMEM((groups * cols, QUAD * tok), F32)],
    )(rank1, *normed, *weights)

    got = []
    for x in range(4):
        relay = [
            (i * sections + s, (i ^ x) * sections + (s + 1) % sections)
            for i in range(seq)
            for s in range(sections)
        ]
        got.append(lax.ppermute(pieces[x], ("seq", "section"), relay))
    out = call(
        functools.partial(assemble_kernel, groups, cols, tok),
        "assemble",
        grid=(1,),
        in_specs=[smem] + [full((groups * cols, tok))] * 4,
        out_specs=full((tok, seq * cols)),
        out_shape=shape((tok, seq * cols), BF16),
        scratch_shapes=[pltpu.VMEM((groups * cols, tok), F32), pltpu.VMEM((seq * cols, tok), F32)],
    )(jnp.stack([rank, group]), *got)
    return out[None]


def solution(mesh):
    in_specs = (
        P("section", "seq", None),
        P("section", "seq", None),
        P("section", "seq", None),
        P("section", "seq", None),
        P("section", None, "seq"),
        P("section", None),
        P("section", None, "seq"),
    )
    out_specs = P("section", "seq", None)
    return jax.shard_map(
        per_device, mesh=mesh, in_specs=in_specs, out_specs=out_specs, check_vma=False
    )
```

time: 633 us -> 104 us (0.16)
  waiting for transfers between devices: 353 us -> 53.8 us
  other arithmetic: 176 us -> 0.07 us
  matrix products: 68.2 us -> 0 us
  starting transfers between devices: 0.14 us -> 27 us
  Pallas kernels: 0 us -> 21.5 us
  local copies, waits for them, and re-layouts: 20.2 us -> 0.88 us
  between operations: 13.5 us -> 0.14 us
    all_gather x3 -> x0, waiting for transfers between devices: 343 us -> none  [the longest x2 244 us: prefix_2(): everything = jax.tree.map(lambda part: lax.all_gather(part, axis), shard)]
    another operation x4 -> x1, other arithmetic: 171 us -> 0.07 us  [per_device(): jnp.stack([rank, group])]
    dot_general x25 -> x0, matrix products: 62.8 us -> none  [the longest x10 27.3 us: combine(): jnp.einsum('hde,hef->hdf', later[0], earlier[1], precision=exact_precision)]
    ppermute x1 -> x16, waiting for transfers between devices: 9.29 us -> 53.8 us  [the longest x9 32.2 us: near(): return lax.ppermute(value, 'seq', [(i, i ^ x) for i in range(seq)])]
    ppermute x1 -> x16, starting transfers between devices: 0.06 us -> 27 us  [the longest x9 13 us: near(): return lax.ppermute(value, 'seq', [(i, i ^ x) for i in range(seq)])]
    pallas_call x0 -> x8, Pallas kernels: none -> 21.5 us  [the longest x1 9.57 us: per_device(): call(functools.partial(maps_kernel, two, tok, more), 'maps', limit=32, gr...]
    while x37 -> x0, local copies, waits for them, and re-layouts: 9.5 us -> none
  transfers between devices with their start and end apart: 4 -> 16, of which waited for: 4 -> 10; matrix products, arithmetic and copies ran while one was open for 7% -> 0% of each run, Pallas kernels for 0% -> 15%
where the time goes in v2:
time: 104 us; the launch traced here: 103 us
  waiting for transfers between devices  53.8 us (52%)
  starting transfers between devices  27 us (26%)
  Pallas kernels  21.5 us (21%)
    ppermute x9, waiting for transfers between devices, near(): return lax.ppermute(value, 'seq', [(i, i ^ x) for i in range(seq)])  32.2 us
    ppermute x2, waiting for transfers between devices, send_part(): lax.ppermute(part, 'seq', [(j, (j + g * QUAD) % seq) for j in range(seq)])  13.6 us
    ppermute x9, starting transfers between devices, near(): return lax.ppermute(value, 'seq', [(i, i ^ x) for i in range(seq)])  13 us
    pallas_call x1, Pallas kernels, per_device(): call(functools.partial(maps_kernel, two, tok, more), 'maps', limit=32, gr...  9.57 us
    ppermute x4, waiting for transfers between devices, per_device(): got.append(lax.ppermute(pieces[x], ('seq', 'section'), relay))  7.99 us
    ppermute x2, starting transfers between devices, send_part(): lax.ppermute(part, 'seq', [(j, (j + g * QUAD) % seq) for j in range(seq)])  5.76 us
    ppermute x4, starting transfers between devices, per_device(): got.append(lax.ppermute(pieces[x], ('seq', 'section'), relay))  4.43 us
    ppermute x1, starting transfers between devices, per_device(): start = lax.ppermute(total, 'seq', onward)  3.8 us
  transfers between devices with their start and end apart: 16, of which 10 were waited for; matrix products, arithmetic and copies ran while one was open for 0% of the time, Pallas kernels for 15%

profile of v2, /device:TPU:0, one launch (start us, length us, event | category | flops | bytes accessed | tf_op | source)
XLA Modules:
  0.0 103.4 jit_solution(14895522254206275414)
XLA Ops:
  0.8 1.4 %pack_kl.1 = (bf16[272,512]{1,0:T(8,128)(2,1)S(1)}, bf16[272,512]{1,0:T(8,128)(2,1)S(1)}, bf16[272,512]{1,0:T(8,128)(2,1)S(1)}, bf16[272,512]{1,0:T(8,128)(2,1)S(1)}) custom-call(s32[1]{0:T(128)} %bitcast.rank_ref, bf16[128,2048]{1,0:T(8,128)(2,1)} %bitcast.15, bf16[128,2048]{1,0:T(8,128)(2,1)} %bitcast.16, f32[16,128]{1,0:T(8,128)S(1)} %bitcast.14), custom_call_target="tpu_custom_call" | custom-call | tf_op jit(solution)/shard_map/pack_kl/pallas_call | solution.py:293
  2.2 3.0 %collective-permute-start = (bf16[272,512]{1,0:T(8,128)(2,1)S(1)}, bf16[272,512]{1,0:T(8,128)(2,1)S(1)}, u32[]{:S(2)}, u32[]{:S(2)}) collective-permute-start(bf16[272,512]{1,0:T(8,128)(2,1)S(1)} %get-tuple-element.41), channel_id=1, source_target_pairs={{0,4},{4,0},{8,12},{12,8},{16,20},{20,16},{24,28},{28,24},{1,5},{5... | collective-permute-start | bytes 835592 | tf_op jit(solution)/shard_map/ppermute | solution.py:288
  5.2 1.6 %collective-permute-start.1 = (bf16[272,512]{1,0:T(8,128)(2,1)S(1)}, bf16[272,512]{1,0:T(8,128)(2,1)S(1)}, u32[]{:S(2)}, u32[]{:S(2)}) collective-permute-start(bf16[272,512]{1,0:T(8,128)(2,1)S(1)} %get-tuple-element.42), channel_id=1, source_target_pairs={{0,8},{4,12},{8,0},{12,4},{16,24},{20,28},{24,16},{28,20},{1,9},{5... | collective-permute-start | bytes 835592 | tf_op jit(solution)/shard_map/ppermute | solution.py:288
  6.8 1.4 %pack_vq.1 = (bf16[256,512]{1,0:T(8,128)(2,1)S(1)}, bf16[256,512]{1,0:T(8,128)(2,1)S(1)}, bf16[256,512]{1,0:T(8,128)(2,1)S(1)}, bf16[256,512]{1,0:T(8,128)(2,1)S(1)}) custom-call(s32[1]{0:T(128)} %bitcast.rank_ref, bf16[128,2048]{1,0:T(8,128)(2,1)} %bitcast.17, bf16[128,2048]{1,0:T(8,128)(2,1)} %bitcast.18), custom_call_target="tpu_custom_call" | custom-call | tf_op jit(solution)/shard_map/pack_vq/pallas_call | solution.py:300
  8.1 3.7 %collective-permute-done.refs_1_ = bf16[272,512]{1,0:T(8,128)(2,1)S(1)} collective-permute-done((bf16[272,512]{1,0:T(8,128)(2,1)S(1)}, bf16[272,512]{1,0:T(8,128)(2,1)S(1)}, u32[]{:S(2)}, u32[]{:S(2)}) %collective-permute-start) | collective-permute-done | bytes 278560 | tf_op jit(solution)/shard_map/ppermute | solution.py:288
  11.9 2.9 %collective-permute-done.1.refs_2_ = bf16[272,512]{1,0:T(8,128)(2,1)S(1)} collective-permute-done((bf16[272,512]{1,0:T(8,128)(2,1)S(1)}, bf16[272,512]{1,0:T(8,128)(2,1)S(1)}, u32[]{:S(2)}, u32[]{:S(2)}) %collective-permute-start.1) | collective-permute-done | bytes 278560 | tf_op jit(solution)/shard_map/ppermute | solution.py:288
  14.8 2.0 %collective-permute-start.3 = (bf16[256,512]{1,0:T(8,128)(2,1)S(1)}, bf16[256,512]{1,0:T(8,128)(2,1)S(1)}, u32[]{:S(2)}, u32[]{:S(2)}) collective-permute-start(bf16[256,512]{1,0:T(8,128)(2,1)S(1)} %get-tuple-element.44), channel_id=1, source_target_pairs={{0,8},{4,12},{8,0},{12,4},{16,24},{20,28},{24,16},{28,20},{1,9},{5... | collective-permute-start | bytes 786440 | tf_op jit(solution)/shard_map/ppermute | solution.py:288
  16.9 1.4 %collective-permute-start.4 = (bf16[256,512]{1,0:T(8,128)(2,1)S(1)}, bf16[256,512]{1,0:T(8,128)(2,1)S(1)}, u32[]{:S(2)}, u32[]{:S(2)}) collective-permute-start(bf16[256,512]{1,0:T(8,128)(2,1)S(1)} %get-tuple-element.45), channel_id=1, source_target_pairs={{0,12},{4,8},{8,4},{12,0},{16,28},{20,24},{24,20},{28,16},{1,13},{... | collective-permute-start | bytes 786440 | tf_op jit(solution)/shard_map/ppermute | solution.py:288
  18.3 2.7 %collective-permute-start.7 = (bf16[96,2048]{1,0:T(8,128)(2,1)S(1)}, bf16[96,2048]{1,0:T(8,128)(2,1)S(1)}, u32[]{:S(2)}, u32[]{:S(2)}) collective-permute-start(bf16[96,2048]{1,0:T(8,128)(2,1)S(1)} %slice.8), channel_id=1, source_target_pairs={{0,16},{4,20},{8,24},{12,28},{16,0},{20,4},{24,8},{28,12},{1,17},{... | collective-permute-start | bytes 1179656 | tf_op jit(solution)/shard_map/ppermute | solution.py:315
  21.0 7.7 %collective-permute-done.5.refs_3_ = bf16[272,512]{1,0:T(8,128)(2,1)S(1)} collective-permute-done((bf16[272,512]{1,0:T(8,128)(2,1)S(1)}, bf16[272,512]{1,0:T(8,128)(2,1)S(1)}, u32[]{:S(2)}, u32[]{:S(2)}) %collective-permute-start.5) | collective-permute-done | bytes 278560 | tf_op jit(solution)/shard_map/ppermute | solution.py:288
  28.7 9.6 %maps.1 = (bf16[4,4,128,256]{3,2,1,0:T(8,128)(2,1)S(1)}, bf16[4,4,128,256]{3,2,1,0:T(8,128)(2,1)S(1)}, bf16[4,4,128,256]{3,2,1,0:T(8,128)(2,1)S(1)}, bf16[4,4,12...) custom-call(s32[1]{0:T(128)} %bitcast.rank_ref, ...), custom_call_target="tpu_custom_call" | custom-call | tf_op jit(solution)/shard_map/maps/pallas_call | solution.py:335
  39.9 3.8 %collective-permute-start.6 = (bf16[4,128,128]{2,1,0:T(8,128)(2,1)S(1)}, bf16[4,128,128]{2,1,0:T(8,128)(2,1)S(1)}, u32[]{:S(2)}, u32[]{:S(2)}) collective-permute-start(bf16[4,128,128]{2,1,0:T(8,128)(2,1)S(1)} %get-tuple-element.50), channel_id=1, source_target_pairs={{0,16},{4,20},{8,24},{12,28},{1,17},{5,21},{9,25},{13,29},{2,18},{... | collective-permute-start | bytes 393224 | tf_op jit(solution)/shard_map/ppermute | solution.py:356
  43.7 3.7 %local.1 = (bf16[4,4,128,256]{3,2,1,0:T(8,128)(2,1)S(1)}, f32[4,4,128,128]{3,2,1,0:T(8,128)S(1)}) custom-call(s32[1]{0:T(128)} %bitcast.rank_ref, bf16[272,512]{1,0:T(8,128)(2,1)S(1)} %get-tuple-element.46.refs_0_, bf16[272,512]{1,0:T(8,128)(2,1)S(1)} %collective-permute-done.refs_1_, bf16[272,512]{1,0:T(8,128)(2,1)S(1)} %collective-permute-done.1.refs_2_, ...), custom_call_target="tpu_custom_call" | custom-call | tf_op jit(solution)/shard_map/local/pallas_call | solution.py:361
  48.0 2.5 %collective-permute-start.9 = (bf16[512,512]{1,0:T(8,128)(2,1)S(1)}, bf16[512,512]{1,0:T(8,128)(2,1)S(1)}, u32[]{:S(2)}, u32[]{:S(2)}) collective-permute-start(bf16[512,512]{1,0:T(8,128)(2,1)S(1)} %finish.1.refs_0_), channel_id=1, source_target_pairs={{0,8},{4,12},{8,0},{12,4},{16,24},{20,28},{24,16},{28,20},{1,9},{5... | collective-permute-start | bytes 1572872 | tf_op jit(solution)/shard_map/ppermute | solution.py:288
  50.5 3.1 %collective-permute-start.11 = (bf16[192,2048]{1,0:T(8,128)(2,1)S(1)}, bf16[192,2048]{1,0:T(8,128)(2,1)S(1)}, u32[]{:S(2)}, u32[]{:S(2)}) collective-permute-start(bf16[192,2048]{1,0:T(8,128)(2,1)S(1)} %slice.9), channel_id=1, source_target_pairs={{0,16},{4,20},{8,24},{12,28},{16,0},{20,4},{24,8},{28,12},{1,17},{... | collective-permute-start | bytes 2359304 | tf_op jit(solution)/shard_map/ppermute | solution.py:315
  54.7 17.3 %collective-permute-done.9.refs_2_ = bf16[512,512]{1,0:T(8,128)(2,1)S(1)} collective-permute-done((bf16[512,512]{1,0:T(8,128)(2,1)S(1)}, bf16[512,512]{1,0:T(8,128)(2,1)S(1)}, u32[]{:S(2)}, u32[]{:S(2)}) %collective-permute-start.9) | collective-permute-done | bytes 524320 | tf_op jit(solution)/shard_map/ppermute | solution.py:288
  73.3 13.6 %collective-permute-done.11.refs_6_ = bf16[192,2048]{1,0:T(8,128)(2,1)S(1)} collective-permute-done((bf16[192,2048]{1,0:T(8,128)(2,1)S(1)}, bf16[192,2048]{1,0:T(8,128)(2,1)S(1)}, u32[]{:S(2)}, u32[]{:S(2)}) %collective-permute-start.11) | collective-permute-done | bytes 786464 | tf_op jit(solution)/shard_map/ppermute | solution.py:315
  87.0 2.2 %product.1 = (bf16[576,128]{1,0:T(8,128)(2,1)S(1)}, bf16[576,128]{1,0:T(8,128)(2,1)S(1)}, bf16[576,128]{1,0:T(8,128)(2,1)S(1)}, bf16[576,128]{1,0:T(8,128)(2,1)S(1)}) custom-call(s32[1]{0:T(128)} %bitcast.rank_ref, bf16[512,512]{1,0:T(8,128)(2,1)S(1)} %finish.1.refs_0_, bf16[512,512]{1,0:T(8,128)(2,1)S(1)} %collective-permute-done.8.refs_1_, ...), custom_call_target="tpu_custom_call" | custom-call | tf_op jit(solution)/shard_map/product/pallas_call | solution.py:392
  89.3 2.4 %collective-permute-start.13 = (bf16[576,128]{1,0:T(8,128)(2,1)S(1)}, bf16[576,128]{1,0:T(8,128)(2,1)S(1)}, u32[]{:S(2)}, u32[]{:S(2)}) collective-permute-start(bf16[576,128]{1,0:T(8,128)(2,1)S(1)} %get-tuple-element.66), channel_id=1, source_target_pairs={{0,5},{1,6},{2,7},{3,4},{4,1},{5,2},{6,3},{7,0},{8,13},{9,14},{10,... | collective-permute-start | bytes 442376 | tf_op jit(solution)/shard_map/ppermute | solution.py:410
  91.7 2.0 %collective-permute-start.15 = (bf16[576,128]{1,0:T(8,128)(2,1)S(1)}, bf16[576,128]{1,0:T(8,128)(2,1)S(1)}, u32[]{:S(2)}, u32[]{:S(2)}) collective-permute-start(bf16[576,128]{1,0:T(8,128)(2,1)S(1)} %get-tuple-element.68), channel_id=1, source_target_pairs={{0,13},{1,14},{2,15},{3,12},{4,9},{5,10},{6,11},{7,8},{8,5},{9,6},... | collective-permute-start | bytes 442376 | tf_op jit(solution)/shard_map/ppermute | solution.py:410
  93.8 2.5 %collective-permute-done.13.refs_1_ = bf16[576,128]{1,0:T(8,128)(2,1)S(1)} collective-permute-done((bf16[576,128]{1,0:T(8,128)(2,1)S(1)}, bf16[576,128]{1,0:T(8,128)(2,1)S(1)}, u32[]{:S(2)}, u32[]{:S(2)}) %collective-permute-start.13) | collective-permute-done | bytes 147488 | tf_op jit(solution)/shard_map/ppermute | solution.py:410
  96.4 2.3 %collective-permute-done.14.refs_2_ = bf16[576,128]{1,0:T(8,128)(2,1)S(1)} collective-permute-done((bf16[576,128]{1,0:T(8,128)(2,1)S(1)}, bf16[576,128]{1,0:T(8,128)(2,1)S(1)}, u32[]{:S(2)}, u32[]{:S(2)}) %collective-permute-start.14) | collective-permute-done | bytes 147488 | tf_op jit(solution)/shard_map/ppermute | solution.py:410
  98.7 3.0 %collective-permute-done.15.refs_3_ = bf16[576,128]{1,0:T(8,128)(2,1)S(1)} collective-permute-done((bf16[576,128]{1,0:T(8,128)(2,1)S(1)}, bf16[576,128]{1,0:T(8,128)(2,1)S(1)}, u32[]{:S(2)}, u32[]{:S(2)}) %collective-permute-start.15) | collective-permute-done | bytes 147488 | tf_op jit(solution)/shard_map/ppermute | solution.py:410
  101.7 1.7 %assemble.1 = bf16[128,2304]{1,0:T(8,128)(2,1)} custom-call(s32[2]{0:T(128)S(1)} %pad_add_fusion.place_ref, bf16[576,128]{1,0:T(8,128)(2,1)S(1)} %collective-permute-done.12.refs_0_, bf16[576,128]{1,0:T(8,128)(2,1)S(1)} %collective-permute-done.13.refs_1_, bf16[576,128]{1,0:T(8,128)(2,1)S(1)} %collective-permute-done.14.refs_2_, ...), custom_call_target="tpu_custom_call" | custom-call | tf_op jit(solution)/shard_map/assemble/pallas_call | solution.py:411
  (25 shorter events, 5.7 us)
Async XLA Ops:
  0.0 18.3 %copy-start = (bf16[1,2048,288]{1,2,0:T(8,128)(2,1)S(1)}, bf16[1,2048,288]{1,2,0:T(8,128)(2,1)}, u32[]{:S(2)}) copy-start(bf16[1,2048,288]{1,2,0:T(8,128)(2,1)} %param.13) | copy-start | bytes 3538948
  0.0 0.8 copy-start.1
  2.2 9.7 %collective-permute-start = (bf16[272,512]{1,0:T(8,128)(2,1)S(1)}, bf16[272,512]{1,0:T(8,128)(2,1)S(1)}, u32[]{:S(2)}, u32[]{:S(2)}) collective-permute-start(bf16[272,512]{1,0:T(8,128)(2,1)S(1)} %get-tuple-element.41), channel_id=1, source_target_pairs={{0,4},{4,0},{8,12},{12,8},{16,20},{20,16},{24,28},{28,24},{1,5},{5... | collective-permute-start | bytes 835592 | tf_op jit(solution)/shard_map/ppermute | solution.py:288
  5.2 9.6 %collective-permute-start.1 = (bf16[272,512]{1,0:T(8,128)(2,1)S(1)}, bf16[272,512]{1,0:T(8,128)(2,1)S(1)}, u32[]{:S(2)}, u32[]{:S(2)}) collective-permute-start(bf16[272,512]{1,0:T(8,128)(2,1)S(1)} %get-tuple-element.42), channel_id=1, source_target_pairs={{0,8},{4,12},{8,0},{12,4},{16,24},{20,28},{24,16},{28,20},{1,9},{5... | collective-permute-start | bytes 835592 | tf_op jit(solution)/shard_map/ppermute | solution.py:288
  6.8 21.9 %collective-permute-start.5 = (bf16[272,512]{1,0:T(8,128)(2,1)S(1)}, bf16[272,512]{1,0:T(8,128)(2,1)S(1)}, u32[]{:S(2)}, u32[]{:S(2)}) collective-permute-start(bf16[272,512]{1,0:T(8,128)(2,1)S(1)} %get-tuple-element.47), channel_id=1, source_target_pairs={{0,12},{4,8},{8,4},{12,0},{16,28},{20,24},{24,20},{28,16},{1,13},{... | collective-permute-start | bytes 835592 | tf_op jit(solution)/shard_map/ppermute | solution.py:288
  14.8 23.5 %collective-permute-start.2 = (bf16[256,512]{1,0:T(8,128)(2,1)S(1)}, bf16[256,512]{1,0:T(8,128)(2,1)S(1)}, u32[]{:S(2)}, u32[]{:S(2)}) collective-permute-start(bf16[256,512]{1,0:T(8,128)(2,1)S(1)} %get-tuple-element.43), channel_id=1, source_target_pairs={{0,4},{4,0},{8,12},{12,8},{16,20},{20,16},{24,28},{28,24},{1,5},{5... | collective-permute-start | bytes 786440 | tf_op jit(solution)/shard_map/ppermute | solution.py:288
  14.8 23.5 %collective-permute-start.3 = (bf16[256,512]{1,0:T(8,128)(2,1)S(1)}, bf16[256,512]{1,0:T(8,128)(2,1)S(1)}, u32[]{:S(2)}, u32[]{:S(2)}) collective-permute-start(bf16[256,512]{1,0:T(8,128)(2,1)S(1)} %get-tuple-element.44), channel_id=1, source_target_pairs={{0,8},{4,12},{8,0},{12,4},{16,24},{20,28},{24,16},{28,20},{1,9},{5... | collective-permute-start | bytes 786440 | tf_op jit(solution)/shard_map/ppermute | solution.py:288
  16.9 21.9 %collective-permute-start.4 = (bf16[256,512]{1,0:T(8,128)(2,1)S(1)}, bf16[256,512]{1,0:T(8,128)(2,1)S(1)}, u32[]{:S(2)}, u32[]{:S(2)}) collective-permute-start(bf16[256,512]{1,0:T(8,128)(2,1)S(1)} %get-tuple-element.45), channel_id=1, source_target_pairs={{0,12},{4,8},{8,4},{12,0},{16,28},{20,24},{24,20},{28,16},{1,13},{... | collective-permute-start | bytes 786440 | tf_op jit(solution)/shard_map/ppermute | solution.py:288
  18.3 29.1 %collective-permute-start.7 = (bf16[96,2048]{1,0:T(8,128)(2,1)S(1)}, bf16[96,2048]{1,0:T(8,128)(2,1)S(1)}, u32[]{:S(2)}, u32[]{:S(2)}) collective-permute-start(bf16[96,2048]{1,0:T(8,128)(2,1)S(1)} %slice.8), channel_id=1, source_target_pairs={{0,16},{4,20},{8,24},{12,28},{16,0},{20,4},{24,8},{28,12},{1,17},{... | collective-permute-start | bytes 1179656 | tf_op jit(solution)/shard_map/ppermute | solution.py:315
  39.9 7.5 %collective-permute-start.6 = (bf16[4,128,128]{2,1,0:T(8,128)(2,1)S(1)}, bf16[4,128,128]{2,1,0:T(8,128)(2,1)S(1)}, u32[]{:S(2)}, u32[]{:S(2)}) collective-permute-start(bf16[4,128,128]{2,1,0:T(8,128)(2,1)S(1)} %get-tuple-element.50), channel_id=1, source_target_pairs={{0,16},{4,20},{8,24},{12,28},{1,17},{5,21},{9,25},{13,29},{2,18},{... | collective-permute-start | bytes 393224 | tf_op jit(solution)/shard_map/ppermute | solution.py:356
  43.7 3.7 %copy-start.2 = (f32[1,2048]{1,0:T(1,128)S(1)}, f32[1,2048]{1,0:T(1,128)}, u32[]{:S(2)}) copy-start(f32[1,2048]{1,0:T(1,128)} %gain_ref.1) | copy-start | bytes 24580
  48.0 24.0 %collective-permute-start.9 = (bf16[512,512]{1,0:T(8,128)(2,1)S(1)}, bf16[512,512]{1,0:T(8,128)(2,1)S(1)}, u32[]{:S(2)}, u32[]{:S(2)}) collective-permute-start(bf16[512,512]{1,0:T(8,128)(2,1)S(1)} %finish.1.refs_0_), channel_id=1, source_target_pairs={{0,8},{4,12},{8,0},{12,4},{16,24},{20,28},{24,16},{28,20},{1,9},{5... | collective-permute-start | bytes 1572872 | tf_op jit(solution)/shard_map/ppermute | solution.py:288
  50.5 36.5 %collective-permute-start.11 = (bf16[192,2048]{1,0:T(8,128)(2,1)S(1)}, bf16[192,2048]{1,0:T(8,128)(2,1)S(1)}, u32[]{:S(2)}, u32[]{:S(2)}) collective-permute-start(bf16[192,2048]{1,0:T(8,128)(2,1)S(1)} %slice.9), channel_id=1, source_target_pairs={{0,16},{4,20},{8,24},{12,28},{16,0},{20,4},{24,8},{28,12},{1,17},{... | collective-permute-start | bytes 2359304 | tf_op jit(solution)/shard_map/ppermute | solution.py:315
  53.6 19.7 %collective-permute-start.8 = (bf16[512,512]{1,0:T(8,128)(2,1)S(1)}, bf16[512,512]{1,0:T(8,128)(2,1)S(1)}, u32[]{:S(2)}, u32[]{:S(2)}) collective-permute-start(bf16[512,512]{1,0:T(8,128)(2,1)S(1)} %finish.1.refs_0_), channel_id=1, source_target_pairs={{0,4},{4,0},{8,12},{12,8},{16,20},{20,16},{24,28},{28,24},{1,5},{5... | collective-permute-start | bytes 1572872 | tf_op jit(solution)/shard_map/ppermute | solution.py:288
  72.0 15.0 %collective-permute-start.10 = (bf16[512,512]{1,0:T(8,128)(2,1)S(1)}, bf16[512,512]{1,0:T(8,128)(2,1)S(1)}, u32[]{:S(2)}, u32[]{:S(2)}) collective-permute-start(bf16[512,512]{1,0:T(8,128)(2,1)S(1)} %collective-permute-done.9.refs_2_), channel_id=1, source_target_pairs={{0,4},{4,0},{8,12},{12,8},{16,20},{20,16},{24,28},{28,24},{1,5},{5... | collective-permute-start | bytes 1572872 | tf_op jit(solution)/shard_map/ppermute | solution.py:288
  89.2 4.6 %collective-permute-start.12 = (bf16[576,128]{1,0:T(8,128)(2,1)S(1)}, bf16[576,128]{1,0:T(8,128)(2,1)S(1)}, u32[]{:S(2)}, u32[]{:S(2)}) collective-permute-start(bf16[576,128]{1,0:T(8,128)(2,1)S(1)} %get-tuple-element.65), channel_id=1, source_target_pairs={{0,1},{1,2},{2,3},{3,0},{4,5},{5,6},{6,7},{7,4},{8,9},{9,10},{10,1... | collective-permute-start | bytes 442376 | tf_op jit(solution)/shard_map/ppermute | solution.py:410
  89.3 7.1 %collective-permute-start.13 = (bf16[576,128]{1,0:T(8,128)(2,1)S(1)}, bf16[576,128]{1,0:T(8,128)(2,1)S(1)}, u32[]{:S(2)}, u32[]{:S(2)}) collective-permute-start(bf16[576,128]{1,0:T(8,128)(2,1)S(1)} %get-tuple-element.66), channel_id=1, source_target_pairs={{0,5},{1,6},{2,7},{3,4},{4,1},{5,2},{6,3},{7,0},{8,13},{9,14},{10,... | collective-permute-start | bytes 442376 | tf_op jit(solution)/shard_map/ppermute | solution.py:410
  91.7 7.0 %collective-permute-start.14 = (bf16[576,128]{1,0:T(8,128)(2,1)S(1)}, bf16[576,128]{1,0:T(8,128)(2,1)S(1)}, u32[]{:S(2)}, u32[]{:S(2)}) collective-permute-start(bf16[576,128]{1,0:T(8,128)(2,1)S(1)} %get-tuple-element.67), channel_id=1, source_target_pairs={{0,9},{1,10},{2,11},{3,8},{4,13},{5,14},{6,15},{7,12},{8,1},{9,2},... | collective-permute-start | bytes 442376 | tf_op jit(solution)/shard_map/ppermute | solution.py:410
  91.7 10.1 %collective-permute-start.15 = (bf16[576,128]{1,0:T(8,128)(2,1)S(1)}, bf16[576,128]{1,0:T(8,128)(2,1)S(1)}, u32[]{:S(2)}, u32[]{:S(2)}) collective-permute-start(bf16[576,128]{1,0:T(8,128)(2,1)S(1)} %get-tuple-element.68), channel_id=1, source_target_pairs={{0,13},{1,14},{2,15},{3,12},{4,9},{5,10},{6,11},{7,8},{8,5},{9,6},... | collective-permute-start | bytes 442376 | tf_op jit(solution)/shard_map/ppermute | solution.py:410

commit v3 on v2

--- a/solution.py
+++ b/solution.py
@@ -105,15 +105,13 @@
 
 
 def pack_vq(tok, width, rank_ref, v_ref, q_ref, *refs):
-    outs, sem = refs[:4], refs[4]
+    outs, sem = refs[:8], refs[8]
     rank = rank_ref[0]
     copies = []
-    for x in range(4):
-        at = pl.multiple_of((rank ^ x) * width, width)
-        for i, source in enumerate((v_ref, q_ref)):
-            copy = pltpu.make_async_copy(
-                source.at[:, pl.ds(at, width)], outs[x].at[i * tok : (i + 1) * tok, :], sem.at[2 * x + i]
-            )
+    for i, source in enumerate((v_ref, q_ref)):
+        for x in range(4):
+            at = pl.multiple_of((rank ^ x) * width, width)
+            copy = pltpu.make_async_copy(source.at[:, pl.ds(at, width)], outs[4 * i + x], sem.at[4 * i + x])
             copy.start()
             copies.append(copy)
     for copy in copies:
@@ -187,15 +185,15 @@
 
 
 def local_kernel(nh, n, rank_ref, *refs):
-    kl, vq = refs[0:4], refs[4:8]
-    inverse_ref, key_ref, shrunk_ref, before_ref, state_ref, query_ref, core_ref = refs[8:]
+    kl, v, q = refs[0:4], refs[4:8], refs[8:12]
+    inverse_ref, key_ref, shrunk_ref, before_ref, state_ref, query_ref, core_ref = refs[12:]
     rank = rank_ref[0]
     row, col = iotas(n)
     tri = (row >= col).astype(BF16)
     every = range(4 * nh)
     at = [(i // 4, i % 4) for i in every]
-    value = chunks_of(vq, rank, slice(0, n), nh, n)
-    query = [x.astype(F32) for x in chunks_of(vq, rank, slice(n, 2 * n), nh, n)]
+    value = chunks_of(v, rank, slice(0, n), nh, n)
+    query = [x.astype(F32) for x in chunks_of(q, rank, slice(0, n), nh, n)]
     cum = [dot1(tri, l) for l in chunks_of(kl, rank, slice(n, 2 * n), nh, n)]
     mid = [c[n // 2 - 1 : n // 2] for c in cum]
     solved = [split(dot2(load_split(inverse_ref, at[i]), value[i])) for i in every]
@@ -301,7 +299,7 @@
         functools.partial(pack_vq, tok, width),
         "pack_vq",
         in_specs=[smem, anywhere, anywhere],
-        out_shape=[shape((2 * tok, width), BF16)] * 4,
+        out_shape=[shape((tok, width), BF16)] * 8,
         scratch_shapes=[pltpu.SemaphoreType.DMA((8,))],
     )(rank1, in_hbm(v), in_hbm(q))
     kl = [kl[0]] + [near(kl[x], x) for x in range(1, 4)]
@@ -321,13 +319,13 @@
         weights[at] = parts
         return values
 
-    vq_1, vq_2, vq_3, *_ = lax.optimization_barrier((*vq[1:], kl[1], kl[2]))
-    vq = [vq[0], near(vq_1, 1), near(vq_2, 2), near(vq_3, 3)]
+    v_1, v_2, v_3, *_ = lax.optimization_barrier((*vq[1:4], kl[1], kl[2]))
+    v_all = [vq[0], near(v_1, 1), near(v_2, 2), near(v_3, 3)]
     send_part(0, kl[1], kl[2])
 
     two = 2
     kl_spec = pl.BlockSpec((2 * tok + 16, two * dk), lambda h: (0, h))
-    vq_spec = pl.BlockSpec((2 * tok, two * dk), lambda h: (0, h))
+    vq_spec = pl.BlockSpec((tok, two * dk), lambda h: (0, h))
     v_spec = pl.BlockSpec((tok, hq * dk), lambda h: (0, h))
     pair = lambda count: pl.BlockSpec((two, count, tok, 2 * dk), lambda h: (h, 0, 0, 0))
     pairs = lambda count: shape((hq, count, tok, 2 * dk), BF16)
@@ -341,6 +339,8 @@
         out_specs=[pair(4)] * 5 + [pair(3)] + [pl.BlockSpec((two, dk, dk), lambda h: (h, 0, 0))] * more,
         out_shape=[pairs(4)] * 5 + [pairs(3)] + [shape((hq, dk, dk), F32)] * more,
     )(rank1, *kl)
+    q_1, q_2, q_3, *_ = lax.optimization_barrier((*vq[5:], inverse))
+    q_all = [vq[4], near(q_1, 1), near(q_2, 2), near(q_3, 3)]
     all4 = lambda count: full((hq, count, tok, 2 * dk))
     states, total = call(
         functools.partial(states_kernel, hq, tok),
@@ -350,7 +350,7 @@
         in_specs=[smem] + [v_spec] * 4 + [all4(4)] * 2,
         out_specs=[all4(3), full((hq, dk, dk))],
         out_shape=[pairs(3), shape((hq, dk, dk), F32 if more else BF16)],
-    )(rank1, *vq, offset, maps)
+    )(rank1, *v_all, offset, maps)
 
     onward = [(i, i + QUAD) for i in range(seq - QUAD)]
     start = lax.ppermute(total, "seq", onward)
@@ -363,10 +363,10 @@
         "local",
         limit=32,
         grid=(hq // two,),
-        in_specs=[smem] + [kl_spec] * 4 + [vq_spec] * 4 + [pair(4)] * 3 + [pair(3)] * 2,
+        in_specs=[smem] + [kl_spec] * 4 + [vq_spec] * 8 + [pair(4)] * 3 + [pair(3)] * 2,
         out_specs=[pair(4), pl.BlockSpec((two, 4, tok, dk), lambda h: (h, 0, 0, 0))],
         out_shape=[pairs(4), shape((hq, 4, tok, dk), F32)],
-    )(rank1, *kl, *vq, inverse, key, shrunk, before, states)
+    )(rank1, *kl, *v_all, *q_all, inverse, key, shrunk, before, states)
     start, core = lax.optimization_barrier((start, core))
     start, core = wait_for(0, start, core)
     send_part(1, start)

time: 104 us -> 99.4 us (0.956)
  waiting for transfers between devices: 53.8 us -> 46.6 us
  starting transfers between devices: 27 us -> 29 us
    ppermute x9 -> x12, waiting for transfers between devices: 32.2 us -> 26.3 us  [near(): return lax.ppermute(value, 'seq', [(i, i ^ x) for i in range(seq)])]
    ppermute x9 -> x12, starting transfers between devices: 13 us -> 17.6 us  [near(): return lax.ppermute(value, 'seq', [(i, i ^ x) for i in range(seq)])]
    ppermute x1, starting transfers between devices: 3.8 us -> 2.24 us  [per_device(): start = lax.ppermute(total, 'seq', onward)]
    ppermute x2, starting transfers between devices: 5.76 us -> 4.72 us  [send_part(): lax.ppermute(part, 'seq', [(j, (j + g * QUAD) % seq) for j in range(seq)])]
  transfers between devices with their start and end apart: 16 -> 19, of which waited for: 10 -> 11; matrix products, arithmetic and copies ran while one was open for 0% -> 1% of each run, Pallas kernels for 15% -> 16%
where the time goes in v3:
time: 99.4 us; the launch traced here: 99.1 us
  waiting for transfers between devices  46.6 us (47%)
  starting transfers between devices  29 us (29%)
  Pallas kernels  21.5 us (22%)
  local copies, waits for them, and re-layouts  1.8 us (2%)
    ppermute x12, waiting for transfers between devices, near(): return lax.ppermute(value, 'seq', [(i, i ^ x) for i in range(seq)])  26.3 us
    ppermute x12, starting transfers between devices, near(): return lax.ppermute(value, 'seq', [(i, i ^ x) for i in range(seq)])  17.6 us
    ppermute x2, waiting for transfers between devices, send_part(): lax.ppermute(part, 'seq', [(j, (j + g * QUAD) % seq) for j in range(seq)])  12.7 us
    pallas_call x1, Pallas kernels, per_device(): call(functools.partial(maps_kernel, two, tok, more), 'maps', limit=32, gr...  9.56 us
    ppermute x4, waiting for transfers between devices, per_device(): got.append(lax.ppermute(pieces[x], ('seq', 'section'), relay))  7.63 us
    ppermute x2, starting transfers between devices, send_part(): lax.ppermute(part, 'seq', [(j, (j + g * QUAD) % seq) for j in range(seq)])  4.72 us
    ppermute x4, starting transfers between devices, per_device(): got.append(lax.ppermute(pieces[x], ('seq', 'section'), relay))  4.43 us
    pallas_call x1, Pallas kernels, per_device(): call(functools.partial(local_kernel, two, tok), 'local', limit=32, grid=(...  3.7 us
  transfers between devices with their start and end apart: 19, of which 11 were waited for; matrix products, arithmetic and copies ran while one was open for 1% of the time, Pallas kernels for 16%

profile of v3, /device:TPU:0, one launch (start us, length us, event | category | flops | bytes accessed | tf_op | source)
XLA Modules:
  0.0 99.1 jit_solution(11208794670751174484)
XLA Ops:
  2.1 3.0 %collective-permute-start = (bf16[272,512]{1,0:T(8,128)(2,1)S(1)}, bf16[272,512]{1,0:T(8,128)(2,1)S(1)}, u32[]{:S(2)}, u32[]{:S(2)}) collective-permute-start(bf16[272,512]{1,0:T(8,128)(2,1)S(1)} %get-tuple-element.48), channel_id=1, source_target_pairs={{0,4},{4,0},{8,12},{12,8},{16,20},{20,16},{24,28},{28,24},{1,5},{5... | collective-permute-start | bytes 835592 | tf_op jit(solution)/shard_map/ppermute | solution.py:286
  5.1 1.6 %collective-permute-start.1 = (bf16[272,512]{1,0:T(8,128)(2,1)S(1)}, bf16[272,512]{1,0:T(8,128)(2,1)S(1)}, u32[]{:S(2)}, u32[]{:S(2)}) collective-permute-start(bf16[272,512]{1,0:T(8,128)(2,1)S(1)} %get-tuple-element.49), channel_id=1, source_target_pairs={{0,8},{4,12},{8,0},{12,4},{16,24},{20,28},{24,16},{28,20},{1,9},{5... | collective-permute-start | bytes 835592 | tf_op jit(solution)/shard_map/ppermute | solution.py:286
  7.7 4.1 %collective-permute-done.refs_1_ = bf16[272,512]{1,0:T(8,128)(2,1)S(1)} collective-permute-done((bf16[272,512]{1,0:T(8,128)(2,1)S(1)}, bf16[272,512]{1,0:T(8,128)(2,1)S(1)}, u32[]{:S(2)}, u32[]{:S(2)}) %collective-permute-start) | collective-permute-done | bytes 278560 | tf_op jit(solution)/shard_map/ppermute | solution.py:286
  11.8 2.9 %collective-permute-done.1.refs_2_ = bf16[272,512]{1,0:T(8,128)(2,1)S(1)} collective-permute-done((bf16[272,512]{1,0:T(8,128)(2,1)S(1)}, bf16[272,512]{1,0:T(8,128)(2,1)S(1)}, u32[]{:S(2)}, u32[]{:S(2)}) %collective-permute-start.1) | collective-permute-done | bytes 278560 | tf_op jit(solution)/shard_map/ppermute | solution.py:286
  14.7 2.6 %collective-permute-start.10 = (bf16[96,2048]{1,0:T(8,128)(2,1)S(1)}, bf16[96,2048]{1,0:T(8,128)(2,1)S(1)}, u32[]{:S(2)}, u32[]{:S(2)}) collective-permute-start(bf16[96,2048]{1,0:T(8,128)(2,1)S(1)} %slice.8), channel_id=1, source_target_pairs={{0,16},{4,20},{8,24},{12,28},{16,0},{20,4},{24,8},{28,12},{1,17},{... | collective-permute-start | bytes 1179656 | tf_op jit(solution)/shard_map/ppermute | solution.py:313
  19.2 1.6 %collective-permute-start.3 = (bf16[128,512]{1,0:T(8,128)(2,1)S(1)}, bf16[128,512]{1,0:T(8,128)(2,1)S(1)}, u32[]{:S(2)}, u32[]{:S(2)}) collective-permute-start(bf16[128,512]{1,0:T(8,128)(2,1)S(1)} %get-tuple-element.51), channel_id=1, source_target_pairs={{0,8},{4,12},{8,0},{12,4},{16,24},{20,28},{24,16},{28,20},{1,9},{5... | collective-permute-start | bytes 393224 | tf_op jit(solution)/shard_map/ppermute | solution.py:286
  22.2 3.7 %collective-permute-done.5.refs_3_ = bf16[272,512]{1,0:T(8,128)(2,1)S(1)} collective-permute-done((bf16[272,512]{1,0:T(8,128)(2,1)S(1)}, bf16[272,512]{1,0:T(8,128)(2,1)S(1)}, u32[]{:S(2)}, u32[]{:S(2)}) %collective-permute-start.5) | collective-permute-done | bytes 278560 | tf_op jit(solution)/shard_map/ppermute | solution.py:286
  25.9 9.6 %maps.1 = (bf16[4,4,128,256]{3,2,1,0:T(8,128)(2,1)S(1)}, bf16[4,4,128,256]{3,2,1,0:T(8,128)(2,1)S(1)}, bf16[4,4,128,256]{3,2,1,0:T(8,128)(2,1)S(1)}, bf16[4,4,12...) custom-call(s32[1]{0:T(128)} %bitcast.rank_ref, ...), custom_call_target="tpu_custom_call" | custom-call | tf_op jit(solution)/shard_map/maps/pallas_call | solution.py:333
  35.5 2.2 %collective-permute-start.7 = (bf16[128,512]{1,0:T(8,128)(2,1)S(1)}, bf16[128,512]{1,0:T(8,128)(2,1)S(1)}, u32[]{:S(2)}, u32[]{:S(2)}) collective-permute-start(bf16[128,512]{1,0:T(8,128)(2,1)S(1)} %get-tuple-element.63), channel_id=1, source_target_pairs={{0,4},{4,0},{8,12},{12,8},{16,20},{20,16},{24,28},{28,24},{1,5},{5... | collective-permute-start | bytes 393224 | tf_op jit(solution)/shard_map/ppermute | solution.py:286
  37.7 1.5 %collective-permute-start.9 = (bf16[128,512]{1,0:T(8,128)(2,1)S(1)}, bf16[128,512]{1,0:T(8,128)(2,1)S(1)}, u32[]{:S(2)}, u32[]{:S(2)}) collective-permute-start(bf16[128,512]{1,0:T(8,128)(2,1)S(1)} %get-tuple-element.65), channel_id=1, source_target_pairs={{0,12},{4,8},{8,4},{12,0},{16,28},{20,24},{24,20},{28,16},{1,13},{... | collective-permute-start | bytes 393224 | tf_op jit(solution)/shard_map/ppermute | solution.py:286
  40.4 2.2 %collective-permute-start.6 = (bf16[4,128,128]{2,1,0:T(8,128)(2,1)S(1)}, bf16[4,128,128]{2,1,0:T(8,128)(2,1)S(1)}, u32[]{:S(2)}, u32[]{:S(2)}) collective-permute-start(bf16[4,128,128]{2,1,0:T(8,128)(2,1)S(1)} %get-tuple-element.57), channel_id=1, source_target_pairs={{0,16},{4,20},{8,24},{12,28},{1,17},{5,21},{9,25},{13,29},{2,18},{... | collective-permute-start | bytes 393224 | tf_op jit(solution)/shard_map/ppermute | solution.py:356
  43.7 3.7 %local.1 = (bf16[4,4,128,256]{3,2,1,0:T(8,128)(2,1)S(1)}, f32[4,4,128,128]{3,2,1,0:T(8,128)S(1)}) custom-call(s32[1]{0:T(128)} %bitcast.rank_ref, bf16[272,512]{1,0:T(8,128)(2,1)S(1)} %get-tuple-element.53.refs_0_, bf16[272,512]{1,0:T(8,128)(2,1)S(1)} %collective-permute-done.refs_1_, bf16[272,512]{1,0:T(8,128)(2,1)S(1)} %collective-permute-done.1.refs_2_, ...), custom_call_target="tpu_custom_call" | custom-call | tf_op jit(solution)/shard_map/local/pallas_call | solution.py:361
  48.0 2.0 %collective-permute-start.12 = (bf16[512,512]{1,0:T(8,128)(2,1)S(1)}, bf16[512,512]{1,0:T(8,128)(2,1)S(1)}, u32[]{:S(2)}, u32[]{:S(2)}) collective-permute-start(bf16[512,512]{1,0:T(8,128)(2,1)S(1)} %finish.1.refs_0_), channel_id=1, source_target_pairs={{0,8},{4,12},{8,0},{12,4},{16,24},{20,28},{24,16},{28,20},{1,9},{5... | collective-permute-start | bytes 1572872 | tf_op jit(solution)/shard_map/ppermute | solution.py:286
  50.1 2.1 %collective-permute-start.14 = (bf16[192,2048]{1,0:T(8,128)(2,1)S(1)}, bf16[192,2048]{1,0:T(8,128)(2,1)S(1)}, u32[]{:S(2)}, u32[]{:S(2)}) collective-permute-start(bf16[192,2048]{1,0:T(8,128)(2,1)S(1)} %slice.9), channel_id=1, source_target_pairs={{0,16},{4,20},{8,24},{12,28},{16,0},{20,4},{24,8},{28,12},{1,17},{... | collective-permute-start | bytes 2359304 | tf_op jit(solution)/shard_map/ppermute | solution.py:313
  53.7 14.5 %collective-permute-done.12.refs_2_ = bf16[512,512]{1,0:T(8,128)(2,1)S(1)} collective-permute-done((bf16[512,512]{1,0:T(8,128)(2,1)S(1)}, bf16[512,512]{1,0:T(8,128)(2,1)S(1)}, u32[]{:S(2)}, u32[]{:S(2)}) %collective-permute-start.12) | collective-permute-done | bytes 524320 | tf_op jit(solution)/shard_map/ppermute | solution.py:286
  68.3 2.1 %collective-permute-start.13 = (bf16[512,512]{1,0:T(8,128)(2,1)S(1)}, bf16[512,512]{1,0:T(8,128)(2,1)S(1)}, u32[]{:S(2)}, u32[]{:S(2)}) collective-permute-start(bf16[512,512]{1,0:T(8,128)(2,1)S(1)} %collective-permute-done.12.refs_2_), channel_id=1, source_target_pairs={{0,4},{4,0},{8,12},{12,8},{16,20},{20,16},{24,28},{28,24},{1,5},{5... | collective-permute-start | bytes 1572872 | tf_op jit(solution)/shard_map/ppermute | solution.py:286
  70.4 12.7 %collective-permute-done.14.refs_6_ = bf16[192,2048]{1,0:T(8,128)(2,1)S(1)} collective-permute-done((bf16[192,2048]{1,0:T(8,128)(2,1)S(1)}, bf16[192,2048]{1,0:T(8,128)(2,1)S(1)}, u32[]{:S(2)}, u32[]{:S(2)}) %collective-permute-start.14) | collective-permute-done | bytes 786464 | tf_op jit(solution)/shard_map/ppermute | solution.py:313
  83.1 2.2 %product.1 = (bf16[576,128]{1,0:T(8,128)(2,1)S(1)}, bf16[576,128]{1,0:T(8,128)(2,1)S(1)}, bf16[576,128]{1,0:T(8,128)(2,1)S(1)}, bf16[576,128]{1,0:T(8,128)(2,1)S(1)}) custom-call(s32[1]{0:T(128)} %bitcast.rank_ref, bf16[512,512]{1,0:T(8,128)(2,1)S(1)} %finish.1.refs_0_, bf16[512,512]{1,0:T(8,128)(2,1)S(1)} %collective-permute-done.11.refs_1_, ...), custom_call_target="tpu_custom_call" | custom-call | tf_op jit(solution)/shard_map/product/pallas_call | solution.py:392
  85.4 1.9 %collective-permute-start.16 = (bf16[576,128]{1,0:T(8,128)(2,1)S(1)}, bf16[576,128]{1,0:T(8,128)(2,1)S(1)}, u32[]{:S(2)}, u32[]{:S(2)}) collective-permute-start(bf16[576,128]{1,0:T(8,128)(2,1)S(1)} %get-tuple-element.80), channel_id=1, source_target_pairs={{0,5},{1,6},{2,7},{3,4},{4,1},{5,2},{6,3},{7,0},{8,13},{9,14},{10,... | collective-permute-start | bytes 442376 | tf_op jit(solution)/shard_map/ppermute | solution.py:410
  87.2 2.5 %collective-permute-start.18 = (bf16[576,128]{1,0:T(8,128)(2,1)S(1)}, bf16[576,128]{1,0:T(8,128)(2,1)S(1)}, u32[]{:S(2)}, u32[]{:S(2)}) collective-permute-start(bf16[576,128]{1,0:T(8,128)(2,1)S(1)} %get-tuple-element.82), channel_id=1, source_target_pairs={{0,13},{1,14},{2,15},{3,12},{4,9},{5,10},{6,11},{7,8},{8,5},{9,6},... | collective-permute-start | bytes 442376 | tf_op jit(solution)/shard_map/ppermute | solution.py:410
  89.9 1.8 %collective-permute-done.16.refs_1_ = bf16[576,128]{1,0:T(8,128)(2,1)S(1)} collective-permute-done((bf16[576,128]{1,0:T(8,128)(2,1)S(1)}, bf16[576,128]{1,0:T(8,128)(2,1)S(1)}, u32[]{:S(2)}, u32[]{:S(2)}) %collective-permute-start.16) | collective-permute-done | bytes 147488 | tf_op jit(solution)/shard_map/ppermute | solution.py:410
  91.7 2.6 %collective-permute-done.17.refs_2_ = bf16[576,128]{1,0:T(8,128)(2,1)S(1)} collective-permute-done((bf16[576,128]{1,0:T(8,128)(2,1)S(1)}, bf16[576,128]{1,0:T(8,128)(2,1)S(1)}, u32[]{:S(2)}, u32[]{:S(2)}) %collective-permute-start.17) | collective-permute-done | bytes 147488 | tf_op jit(solution)/shard_map/ppermute | solution.py:410
  94.3 3.2 %collective-permute-done.18.refs_3_ = bf16[576,128]{1,0:T(8,128)(2,1)S(1)} collective-permute-done((bf16[576,128]{1,0:T(8,128)(2,1)S(1)}, bf16[576,128]{1,0:T(8,128)(2,1)S(1)}, u32[]{:S(2)}, u32[]{:S(2)}) %collective-permute-start.18) | collective-permute-done | bytes 147488 | tf_op jit(solution)/shard_map/ppermute | solution.py:410
  97.4 1.7 %assemble.1 = bf16[128,2304]{1,0:T(8,128)(2,1)} custom-call(s32[2]{0:T(128)S(1)} %pad_add_fusion.place_ref, bf16[576,128]{1,0:T(8,128)(2,1)S(1)} %collective-permute-done.15.refs_0_, bf16[576,128]{1,0:T(8,128)(2,1)S(1)} %collective-permute-done.16.refs_1_, bf16[576,128]{1,0:T(8,128)(2,1)S(1)} %collective-permute-done.17.refs_2_, ...), custom_call_target="tpu_custom_call" | custom-call | tf_op jit(solution)/shard_map/assemble/pallas_call | solution.py:411
  (31 shorter events, 10.9 us)
Async XLA Ops:
  0.0 0.7 copy-start.1
  2.1 9.7 %collective-permute-start = (bf16[272,512]{1,0:T(8,128)(2,1)S(1)}, bf16[272,512]{1,0:T(8,128)(2,1)S(1)}, u32[]{:S(2)}, u32[]{:S(2)}) collective-permute-start(bf16[272,512]{1,0:T(8,128)(2,1)S(1)} %get-tuple-element.48), channel_id=1, source_target_pairs={{0,4},{4,0},{8,12},{12,8},{16,20},{20,16},{24,28},{28,24},{1,5},{5... | collective-permute-start | bytes 835592 | tf_op jit(solution)/shard_map/ppermute | solution.py:286
  5.1 9.6 %collective-permute-start.1 = (bf16[272,512]{1,0:T(8,128)(2,1)S(1)}, bf16[272,512]{1,0:T(8,128)(2,1)S(1)}, u32[]{:S(2)}, u32[]{:S(2)}) collective-permute-start(bf16[272,512]{1,0:T(8,128)(2,1)S(1)} %get-tuple-element.49), channel_id=1, source_target_pairs={{0,8},{4,12},{8,0},{12,4},{16,24},{20,28},{24,16},{28,20},{1,9},{5... | collective-permute-start | bytes 835592 | tf_op jit(solution)/shard_map/ppermute | solution.py:286
  6.7 19.2 %collective-permute-start.5 = (bf16[272,512]{1,0:T(8,128)(2,1)S(1)}, bf16[272,512]{1,0:T(8,128)(2,1)S(1)}, u32[]{:S(2)}, u32[]{:S(2)}) collective-permute-start(bf16[272,512]{1,0:T(8,128)(2,1)S(1)} %get-tuple-element.54), channel_id=1, source_target_pairs={{0,12},{4,8},{8,4},{12,0},{16,28},{20,24},{24,20},{28,16},{1,13},{... | collective-permute-start | bytes 835592 | tf_op jit(solution)/shard_map/ppermute | solution.py:286
  14.7 32.7 %collective-permute-start.10 = (bf16[96,2048]{1,0:T(8,128)(2,1)S(1)}, bf16[96,2048]{1,0:T(8,128)(2,1)S(1)}, u32[]{:S(2)}, u32[]{:S(2)}) collective-permute-start(bf16[96,2048]{1,0:T(8,128)(2,1)S(1)} %slice.8), channel_id=1, source_target_pairs={{0,16},{4,20},{8,24},{12,28},{16,0},{20,4},{24,8},{28,12},{1,17},{... | collective-permute-start | bytes 1179656 | tf_op jit(solution)/shard_map/ppermute | solution.py:313
  18.6 19.1 %collective-permute-start.2 = (bf16[128,512]{1,0:T(8,128)(2,1)S(1)}, bf16[128,512]{1,0:T(8,128)(2,1)S(1)}, u32[]{:S(2)}, u32[]{:S(2)}) collective-permute-start(bf16[128,512]{1,0:T(8,128)(2,1)S(1)} %get-tuple-element.50), channel_id=1, source_target_pairs={{0,4},{4,0},{8,12},{12,8},{16,20},{20,16},{24,28},{28,24},{1,5},{5... | collective-permute-start | bytes 393224 | tf_op jit(solution)/shard_map/ppermute | solution.py:286
  19.2 18.5 %collective-permute-start.3 = (bf16[128,512]{1,0:T(8,128)(2,1)S(1)}, bf16[128,512]{1,0:T(8,128)(2,1)S(1)}, u32[]{:S(2)}, u32[]{:S(2)}) collective-permute-start(bf16[128,512]{1,0:T(8,128)(2,1)S(1)} %get-tuple-element.51), channel_id=1, source_target_pairs={{0,8},{4,12},{8,0},{12,4},{16,24},{20,28},{24,16},{28,20},{1,9},{5... | collective-permute-start | bytes 393224 | tf_op jit(solution)/shard_map/ppermute | solution.py:286
  20.8 18.5 %collective-permute-start.4 = (bf16[128,512]{1,0:T(8,128)(2,1)S(1)}, bf16[128,512]{1,0:T(8,128)(2,1)S(1)}, u32[]{:S(2)}, u32[]{:S(2)}) collective-permute-start(bf16[128,512]{1,0:T(8,128)(2,1)S(1)} %get-tuple-element.52), channel_id=1, source_target_pairs={{0,12},{4,8},{8,4},{12,0},{16,28},{20,24},{24,20},{28,16},{1,13},{... | collective-permute-start | bytes 393224 | tf_op jit(solution)/shard_map/ppermute | solution.py:286
  35.5 7.2 %collective-permute-start.7 = (bf16[128,512]{1,0:T(8,128)(2,1)S(1)}, bf16[128,512]{1,0:T(8,128)(2,1)S(1)}, u32[]{:S(2)}, u32[]{:S(2)}) collective-permute-start(bf16[128,512]{1,0:T(8,128)(2,1)S(1)} %get-tuple-element.63), channel_id=1, source_target_pairs={{0,4},{4,0},{8,12},{12,8},{16,20},{20,16},{24,28},{28,24},{1,5},{5... | collective-permute-start | bytes 393224 | tf_op jit(solution)/shard_map/ppermute | solution.py:286
  37.7 5.0 %collective-permute-start.8 = (bf16[128,512]{1,0:T(8,128)(2,1)S(1)}, bf16[128,512]{1,0:T(8,128)(2,1)S(1)}, u32[]{:S(2)}, u32[]{:S(2)}) collective-permute-start(bf16[128,512]{1,0:T(8,128)(2,1)S(1)} %get-tuple-element.64), channel_id=1, source_target_pairs={{0,8},{4,12},{8,0},{12,4},{16,24},{20,28},{24,16},{28,20},{1,9},{5... | collective-permute-start | bytes 393224 | tf_op jit(solution)/shard_map/ppermute | solution.py:286
  37.7 5.9 %collective-permute-start.9 = (bf16[128,512]{1,0:T(8,128)(2,1)S(1)}, bf16[128,512]{1,0:T(8,128)(2,1)S(1)}, u32[]{:S(2)}, u32[]{:S(2)}) collective-permute-start(bf16[128,512]{1,0:T(8,128)(2,1)S(1)} %get-tuple-element.65), channel_id=1, source_target_pairs={{0,12},{4,8},{8,4},{12,0},{16,28},{20,24},{24,20},{28,16},{1,13},{... | collective-permute-start | bytes 393224 | tf_op jit(solution)/shard_map/ppermute | solution.py:286
  40.4 7.0 %collective-permute-start.6 = (bf16[4,128,128]{2,1,0:T(8,128)(2,1)S(1)}, bf16[4,128,128]{2,1,0:T(8,128)(2,1)S(1)}, u32[]{:S(2)}, u32[]{:S(2)}) collective-permute-start(bf16[4,128,128]{2,1,0:T(8,128)(2,1)S(1)} %get-tuple-element.57), channel_id=1, source_target_pairs={{0,16},{4,20},{8,24},{12,28},{1,17},{5,21},{9,25},{13,29},{2,18},{... | collective-permute-start | bytes 393224 | tf_op jit(solution)/shard_map/ppermute | solution.py:356
  43.6 3.7 %copy-start.2 = (f32[1,2048]{1,0:T(1,128)S(1)}, f32[1,2048]{1,0:T(1,128)}, u32[]{:S(2)}) copy-start(f32[1,2048]{1,0:T(1,128)} %gain_ref.1) | copy-start | bytes 24580
  47.4 2.6 %copy-start = (bf16[1,2048,288]{1,2,0:T(8,128)(2,1)S(1)}, bf16[1,2048,288]{1,2,0:T(8,128)(2,1)}, u32[]{:S(2)}) copy-start(bf16[1,2048,288]{1,2,0:T(8,128)(2,1)} %param.13) | copy-start | bytes 3538948
  48.0 20.3 %collective-permute-start.12 = (bf16[512,512]{1,0:T(8,128)(2,1)S(1)}, bf16[512,512]{1,0:T(8,128)(2,1)S(1)}, u32[]{:S(2)}, u32[]{:S(2)}) collective-permute-start(bf16[512,512]{1,0:T(8,128)(2,1)S(1)} %finish.1.refs_0_), channel_id=1, source_target_pairs={{0,8},{4,12},{8,0},{12,4},{16,24},{20,28},{24,16},{28,20},{1,9},{5... | collective-permute-start | bytes 1572872 | tf_op jit(solution)/shard_map/ppermute | solution.py:286
  50.1 33.0 %collective-permute-start.14 = (bf16[192,2048]{1,0:T(8,128)(2,1)S(1)}, bf16[192,2048]{1,0:T(8,128)(2,1)S(1)}, u32[]{:S(2)}, u32[]{:S(2)}) collective-permute-start(bf16[192,2048]{1,0:T(8,128)(2,1)S(1)} %slice.9), channel_id=1, source_target_pairs={{0,16},{4,20},{8,24},{12,28},{16,0},{20,4},{24,8},{28,12},{1,17},{... | collective-permute-start | bytes 2359304 | tf_op jit(solution)/shard_map/ppermute | solution.py:313
  52.2 18.2 %collective-permute-start.11 = (bf16[512,512]{1,0:T(8,128)(2,1)S(1)}, bf16[512,512]{1,0:T(8,128)(2,1)S(1)}, u32[]{:S(2)}, u32[]{:S(2)}) collective-permute-start(bf16[512,512]{1,0:T(8,128)(2,1)S(1)} %finish.1.refs_0_), channel_id=1, source_target_pairs={{0,4},{4,0},{8,12},{12,8},{16,20},{20,16},{24,28},{28,24},{1,5},{5... | collective-permute-start | bytes 1572872 | tf_op jit(solution)/shard_map/ppermute | solution.py:286
  68.3 14.8 %collective-permute-start.13 = (bf16[512,512]{1,0:T(8,128)(2,1)S(1)}, bf16[512,512]{1,0:T(8,128)(2,1)S(1)}, u32[]{:S(2)}, u32[]{:S(2)}) collective-permute-start(bf16[512,512]{1,0:T(8,128)(2,1)S(1)} %collective-permute-done.12.refs_2_), channel_id=1, source_target_pairs={{0,4},{4,0},{8,12},{12,8},{16,20},{20,16},{24,28},{28,24},{1,5},{5... | collective-permute-start | bytes 1572872 | tf_op jit(solution)/shard_map/ppermute | solution.py:286
  85.3 4.6 %collective-permute-start.15 = (bf16[576,128]{1,0:T(8,128)(2,1)S(1)}, bf16[576,128]{1,0:T(8,128)(2,1)S(1)}, u32[]{:S(2)}, u32[]{:S(2)}) collective-permute-start(bf16[576,128]{1,0:T(8,128)(2,1)S(1)} %get-tuple-element.79), channel_id=1, source_target_pairs={{0,1},{1,2},{2,3},{3,0},{4,5},{5,6},{6,7},{7,4},{8,9},{9,10},{10,1... | collective-permute-start | bytes 442376 | tf_op jit(solution)/shard_map/ppermute | solution.py:410
  85.4 6.3 %collective-permute-start.16 = (bf16[576,128]{1,0:T(8,128)(2,1)S(1)}, bf16[576,128]{1,0:T(8,128)(2,1)S(1)}, u32[]{:S(2)}, u32[]{:S(2)}) collective-permute-start(bf16[576,128]{1,0:T(8,128)(2,1)S(1)} %get-tuple-element.80), channel_id=1, source_target_pairs={{0,5},{1,6},{2,7},{3,4},{4,1},{5,2},{6,3},{7,0},{8,13},{9,14},{10,... | collective-permute-start | bytes 442376 | tf_op jit(solution)/shard_map/ppermute | solution.py:410
  87.2 7.0 %collective-permute-start.17 = (bf16[576,128]{1,0:T(8,128)(2,1)S(1)}, bf16[576,128]{1,0:T(8,128)(2,1)S(1)}, u32[]{:S(2)}, u32[]{:S(2)}) collective-permute-start(bf16[576,128]{1,0:T(8,128)(2,1)S(1)} %get-tuple-element.81), channel_id=1, source_target_pairs={{0,9},{1,10},{2,11},{3,8},{4,13},{5,14},{6,15},{7,12},{8,1},{9,2},... | collective-permute-start | bytes 442376 | tf_op jit(solution)/shard_map/ppermute | solution.py:410
  87.2 10.2 %collective-permute-start.18 = (bf16[576,128]{1,0:T(8,128)(2,1)S(1)}, bf16[576,128]{1,0:T(8,128)(2,1)S(1)}, u32[]{:S(2)}, u32[]{:S(2)}) collective-permute-start(bf16[576,128]{1,0:T(8,128)(2,1)S(1)} %get-tuple-element.82), channel_id=1, source_target_pairs={{0,13},{1,14},{2,15},{3,12},{4,9},{5,10},{6,11},{7,8},{8,5},{9,6},... | collective-permute-start | bytes 442376 | tf_op jit(solution)/shard_map/ppermute | solution.py:410
